TPU v7x, 512 devices: a whole 4x8x8 slice. The times are simulated.
512 devices in a mesh: dp: 4 (over x), expert: 128 (over z, y, core).
Axes of the slice: x: 4, y: 8, z: 8, core: 2. Of those that a mesh axis runs over, the one named last changes fastest.
Arguments:
- tokens: bfloat16 [65536, 1024], P(('dp', 'expert')), may hold values from -6 to 6
- grad_out: bfloat16 [65536, 1024], P(('dp', 'expert')), may hold values from -0.75 to 0.75
- expert_ids: int32 [65536, 4], P(('dp', 'expert')), may hold values from 0 to 127, all different within a row; in each aligned block of 128 rows (0 to 127, 128 to 255, ...) at most 6 rows name the same one
- gate_weight: bfloat16 [65536, 4], P(('dp', 'expert')), may hold values from 0.049804688 to 1
- w_gate: bfloat16 [128, 1024, 384], P('expert'), may hold values from -0.1875 to 0.1875
- w_up: bfloat16 [128, 1024, 384], P('expert'), may hold values from -0.1875 to 0.1875
- w_down: bfloat16 [128, 384, 1024], P('expert'), may hold values from -0.3125 to 0.3125
Outputs:
- grad_tokens: bfloat16 [65536, 1024], P(('dp', 'expert'))
- grad_gate: bfloat16 [65536, 4], P(('dp', 'expert'))
- grad_w_gate: float32 [128, 1024, 384], P('expert', 'dp')
- grad_w_up: float32 [128, 1024, 384], P('expert', 'dp')
- grad_w_down: float32 [128, 384, 1024], P('expert', None, 'dp')
Inputs may be any that keep to these rules, and one draw needn't show every extreme that they name: `expert_ids`: each row names 4 different experts; in the rows of one device no expert is named by more than 6 rows.
All inputs are finite; a program needn't handle non-finite values.
Results may differ from a plain program's by a relative error of at most 0.0085.
Values may be sent and summed in bfloat16 or wider, within the bound.
A program may use at most 64 MiB of HBM per device.

v0:
```python
import jax
import jax.numpy as jnp
from jax import lax
from jax.sharding import PartitionSpec as P


def forward_tile(inputs, weights):
    gate_matrix, up_matrix, down_matrix = weights
    pre_gate = jnp.dot(inputs, gate_matrix, preferred_element_type=jnp.float32)
    pre_up = jnp.dot(inputs, up_matrix, preferred_element_type=jnp.float32)
    hidden = (jax.nn.silu(pre_gate) * pre_up).astype(jnp.bfloat16)
    return (pre_gate, pre_up, hidden)


def backward_tile(inputs, pre_gate, pre_up, hidden, upstream, gate_rows, weights):
    gate_matrix, up_matrix, down_matrix = weights
    across = (((1,), (1,)), ((), ()))
    down_rows = (((0,), (0,)), ((), ()))
    outputs = jnp.dot(hidden, down_matrix, preferred_element_type=jnp.float32)
    upstream_wide = upstream.astype(jnp.float32)
    gate_grad = jnp.sum(outputs * upstream_wide, axis=1).astype(jnp.bfloat16)
    scaled = (gate_rows.astype(jnp.float32)[:, None] * upstream_wide).astype(jnp.bfloat16)
    hidden_grad = lax.dot_general(scaled, down_matrix, across, preferred_element_type=jnp.float32)
    logistic = jax.nn.sigmoid(pre_gate)
    d_gate = (hidden_grad * pre_up * logistic * (1.0 + pre_gate * (1.0 - logistic))).astype(
        jnp.bfloat16
    )
    d_up = (hidden_grad * jax.nn.silu(pre_gate)).astype(jnp.bfloat16)
    route_grad = (
        lax.dot_general(d_gate, gate_matrix, across, preferred_element_type=jnp.float32)
        + lax.dot_general(d_up, up_matrix, across, preferred_element_type=jnp.float32)
    ).astype(jnp.bfloat16)
    grad_terms = (
        lax.dot_general(inputs, d_gate, down_rows, preferred_element_type=jnp.float32),
        lax.dot_general(inputs, d_up, down_rows, preferred_element_type=jnp.float32),
        lax.dot_general(hidden, scaled, down_rows, preferred_element_type=jnp.float32),
    )
    return (route_grad, gate_grad, grad_terms)


def shards(tokens, grad_out, expert_ids, gate_weight, w_gate, w_up, w_down):
    tok_rows, features = tokens.shape
    top_count = expert_ids.shape[1]
    hidden_units = w_gate.shape[2]
    experts = lax.axis_size("expert")
    most_rows = min(tok_rows, 3 * tok_rows * top_count // (2 * experts))
    route_count = tok_rows * top_count
    capacity = experts * most_rows
    route_ids = expert_ids.reshape(route_count)
    onehot = (route_ids[:, None] == jnp.arange(experts, dtype=jnp.int32)[None, :]).astype(jnp.int32)
    before = jnp.sum((jnp.cumsum(onehot, axis=0) - onehot) * onehot, axis=1)
    slot_index = route_ids * most_rows + before
    source = (
        jnp.full((capacity,), route_count, jnp.int32)
        .at[slot_index]
        .set(jnp.arange(route_count, dtype=jnp.int32))
    )
    owner_token = source // top_count
    send_inputs = (
        tokens.at[owner_token].get(mode="fill", fill_value=0).reshape(experts, most_rows, features)
    )
    send_upstream = (
        grad_out.at[owner_token]
        .get(mode="fill", fill_value=0)
        .reshape(experts, most_rows, features)
    )
    send_gates = (
        gate_weight.reshape(route_count)
        .at[source]
        .get(mode="fill", fill_value=0)
        .reshape(experts, most_rows)
    )
    weights = (w_gate[0], w_up[0], w_down[0])
    arrived_inputs, arrived_upstream, arrived_gates = (
        lax.all_to_all(send_inputs, "expert", split_axis=0, concat_axis=0, tiled=True),
        lax.all_to_all(send_upstream, "expert", split_axis=0, concat_axis=0, tiled=True),
        lax.all_to_all(send_gates, "expert", split_axis=0, concat_axis=0, tiled=True),
    )
    inputs = arrived_inputs.reshape(capacity, features)
    gate_rows = arrived_gates.reshape(capacity)
    blocks = 1
    stored = (
        jnp.zeros((capacity, hidden_units), jnp.float32),
        jnp.zeros((capacity, hidden_units), jnp.float32),
        jnp.zeros((capacity, hidden_units), jnp.bfloat16),
    )

    def forward_step(block_index, stored):
        pieces = forward_tile(inputs, weights)
        return tuple((piece for piece in pieces))

    stored = lax.fori_loop(0, blocks, forward_step, stored)
    upstream = arrived_upstream.reshape(capacity, features)
    zero_grads = (
        jnp.zeros((features, hidden_units), jnp.float32),
        jnp.zeros((features, hidden_units), jnp.float32),
        jnp.zeros((hidden_units, features), jnp.float32),
    )
    carry = (
        jnp.zeros((capacity, features), jnp.bfloat16),
        jnp.zeros((capacity,), jnp.bfloat16),
        zero_grads,
    )

    def backward_step(block_index, carry):
        route_grads, gate_grads, grad_sums = carry
        pieces = tuple((whole for whole in stored))
        route_grad, gate_grad, grad_terms = backward_tile(
            inputs, pieces[0], pieces[1], pieces[2], upstream, gate_rows, weights
        )
        route_grads = route_grad
        gate_grads = gate_grad
        grad_sums = tuple((total + term for total, term in zip(grad_sums, grad_terms)))
        return (route_grads, gate_grads, grad_sums)

    route_grads, gate_grads, grad_sums = lax.fori_loop(0, blocks, backward_step, carry)
    back_grads, back_gates = (
        lax.all_to_all(
            route_grads.reshape(experts, most_rows, features),
            "expert",
            split_axis=0,
            concat_axis=0,
            tiled=True,
        ),
        lax.all_to_all(
            gate_grads.reshape(experts, most_rows),
            "expert",
            split_axis=0,
            concat_axis=0,
            tiled=True,
        ),
    )
    per_route = back_grads.reshape(capacity, features)[slot_index].astype(jnp.float32)
    grad_tokens = jnp.sum(per_route.reshape(tok_rows, top_count, features), axis=1).astype(
        jnp.bfloat16
    )
    grad_gate = back_gates.reshape(capacity)[slot_index].reshape(tok_rows, top_count)
    reduced = (
        lax.psum_scatter(
            grad_sums[0].astype(jnp.bfloat16), "dp", scatter_dimension=0, tiled=True
        ).astype(jnp.float32),
        lax.psum_scatter(
            grad_sums[1].astype(jnp.bfloat16), "dp", scatter_dimension=0, tiled=True
        ).astype(jnp.float32),
        lax.psum_scatter(
            grad_sums[2].astype(jnp.bfloat16), "dp", scatter_dimension=1, tiled=True
        ).astype(jnp.float32),
    )
    return (grad_tokens, grad_gate, reduced[0][None], reduced[1][None], reduced[2][None])


def solution(mesh):
    placed = (
        P(("dp", "expert"), None),
        P(("dp", "expert"), None),
        P(("dp", "expert"), None),
        P(("dp", "expert"), None),
        P("expert", None, None),
        P("expert", None, None),
        P("expert", None, None),
    )
    return jax.shard_map(
        shards,
        mesh=mesh,
        in_specs=placed,
        out_specs=(
            P(("dp", "expert"), None),
            P(("dp", "expert"), None),
            P("expert", "dp", None),
            P("expert", "dp", None),
            P("expert", None, "dp"),
        ),
        check_vma=False,
    )
```

profile of v0, /device:TPU:1, one launch (start us, length us, event | category | flops | bytes accessed | tf_op | source)
XLA Modules:
  0.0 298.7 jit_solution(10752991720333486382)
XLA Ops:
  7.2 0.8 broadcast_multiply_fusion
  7.9 0.8 copy.20
  8.9 0.8 copy.24
  10.5 0.2 fusion.15
  10.8 2.4 scatter_custom_fusion
  13.3 5.0 %gather_fusion = bf16[768]{0:T(1024)(128)(2,1)S(1)} fusion(bf16[512]{0:T(512)(128)(2,1)S(1)} %reshape.161, s32[1024]{0:T(1024)S(1)} %pad_clamp_fusion.2), kind=kCustom, calls=%fused_computation | custom fusion | bytes 6144 | tf_op jit(solution)/shard_map/gather | solution.py:70
  18.3 0.8 select_n.54
  19.1 18.4 %all-to-all-start = ((bf16[128,1,6]{2,1,0:T(2,128)(2,1)}), bf16[128,1,6]{2,1,0:T(2,128)(2,1)S(1)}, u32[]{:S(2)}, u32[]{:S(2)}) async-start(bf16[128,1,6]{2,1,0:T(2,128)(2,1)} %select_n.54), calls=%async_computation | async-start | bytes 131072 | tf_op jit(solution)/shard_map/all_to_all | solution.py:77
  37.7 3.6 %gather_fusion.2 = bf16[768,1024]{1,0:T(8,128)(2,1)} fusion(bf16[128,1024]{1,0:T(8,128)(2,1)S(1)} %copy-done.1, s32[1024]{0:T(1024)S(1)} %pad_clamp_fusion.1), kind=kCustom, calls=%fused_computation.2 | custom fusion | bytes 3148800 | tf_op jit(solution)/shard_map/gather | solution.py:60
  41.3 2.5 gather.25
  43.8 3.6 %gather_fusion.1 = bf16[768,1024]{1,0:T(8,128)(2,1)} fusion(bf16[128,1024]{1,0:T(8,128)(2,1)S(1)} %copy-done.2, s32[1024]{0:T(1024)S(1)} %pad_clamp_fusion.1), kind=kCustom, calls=%fused_computation.1 | custom fusion | bytes 3148800 | tf_op jit(solution)/shard_map/gather | solution.py:60
  47.4 3.7 %gather.23 = bf16[128,6,1024]{2,1,0:T(8,128)(2,1)} reshape(bf16[768,1024]{1,0:T(8,128)(2,1)} %gather_fusion.1) | data formatting | bytes 3145728 | tf_op jit(solution)/shard_map/gather | solution.py:60
  51.1 4.0 %broadcast_select_fusion.1 = (bf16[128,6,1024]{2,1,0:T(8,128)(2,1)}, bf16[128,6,1024]{2,1,0:T(8,128)(2,1)}) fusion(bf16[128,6,1024]{2,1,0:T(8,128)(2,1)} %gather.23, pred[128,6]{1,0:T(8,128)(4,1)S(1)} %broadcast_in_dim.40, bf16[128,6,1024]{2,1,0:T(8,128)(2,1)S(1)} %gather.25), kind=kLoop, calls=%fused_computation.11 | loop fusion | flops 1572864 | bytes 6292224 | tf_op jit(solution)/shard_map/select_n | solution.py:60
  55.1 65.0 %all_to_all.27 = bf16[128,6,1024]{2,1,0:T(8,128)(2,1)S(1)} all-to-all(bf16[128,6,1024]{2,1,0:T(8,128)(2,1)} %get-tuple-element.66), channel_id=1, replica_groups=mesh['dp'=4,'expert'=128] {'expert'}, dimensions={0} | all-to-all | bytes 3145728 | tf_op jit(solution)/shard_map/all_to_all | solution.py:76
  120.1 9.3 %all-to-all-start.2 = ((bf16[128,6,1024]{2,1,0:T(8,128)(2,1)}), bf16[128,6,1024]{2,1,0:T(8,128)(2,1)}, u32[]{:S(2)}, u32[]{:S(2)}) async-start(bf16[128,6,1024]{2,1,0:T(8,128)(2,1)} %get-tuple-element.67), calls=%async_computation.2 | async-start | bytes 4194304 | tf_op jit(solution)/shard_map/all_to_all | solution.py:75
  129.6 1.7 multiply_convert_fusion
  131.4 3.7 %convert_element_type.95 = bf16[768,1024]{1,0:T(8,128)(2,1)} reshape(bf16[128,6,1024]{2,1,0:T(8,128)(2,1)} %multiply_convert_fusion) | data formatting | bytes 3145728 | tf_op jit(solution)/shard_map/while/body/eval_jaxpr/convert_element_type | solution.py:22
  135.1 45.2 %all-to-all-done.2 = bf16[128,6,1024]{2,1,0:T(8,128)(2,1)} async-done(((bf16[128,6,1024]{2,1,0:T(8,128)(2,1)}), bf16[128,6,1024]{2,1,0:T(8,128)(2,1)}, u32[]{:S(2)}, u32[]{:S(2)}) %all-to-all-start.2) | async-done | bytes 1572896 | tf_op jit(solution)/shard_map/all_to_all | solution.py:75
  180.2 3.7 %reshape.162 = bf16[768,1024]{1,0:T(8,128)(2,1)} reshape(bf16[128,6,1024]{2,1,0:T(8,128)(2,1)} %all-to-all-done.2) | data formatting | bytes 3145728 | tf_op jit(solution)/shard_map/reshape | solution.py:79
  183.9 2.7 fusion.6
  186.7 1.0 fusion.12
  187.7 0.4 copy-done.3
  188.1 2.2 multiply_convert_fusion.5
  190.3 0.9 copy-done.7
  191.2 1.9 convolution_convert_fusion.1
  193.1 1.9 reshape.168
  195.0 3.3 %multiply_reduce_fusion = bf16[768]{0:T(1024)(128)(2,1)S(1)} fusion(f32[768,1024]{1,0:T(8,128)} %reshape.168, bf16[768,384]{1,0:T(8,128)(2,1)S(1)} %get-tuple-element.63, bf16[1,384,1024]{2,1,0:T(8,128)(2,1)} %param.13), kind=kOutput, calls=%fused_computation.8 | convolution fusion | flops 605551872 | bytes 4523520 | tf_op jit(solution)/shard_map/while/body/eval_jaxpr/dot_general | solution.py:19
  198.3 0.8 convert_element_type.113
  199.1 8.8 %all-to-all-start.4 = ((bf16[128,1,6]{2,1,0:T(2,128)(2,1)}), bf16[128,1,6]{2,1,0:T(2,128)(2,1)S(1)}, u32[]{:S(2)}, u32[]{:S(2)}) async-start(bf16[128,1,6]{2,1,0:T(2,128)(2,1)} %convert_element_type.113), calls=%async_computation.4 | async-start | bytes 131072 | tf_op jit(solution)/shard_map/all_to_all | solution.py:125
  208.0 3.0 %convolution_convert_fusion = bf16[1024,384]{1,0:T(8,128)(2,1)} fusion(bf16[768,1024]{1,0:T(8,128)(2,1)S(1)} %copy-done.4, bf16[768,384]{1,0:T(8,128)(2,1)} %get-tuple-element.65), kind=kOutput, calls=%fused_computation.15 | convolution fusion | flops 604372992 | bytes 2949120 | tf_op jit(solution)/shard_map/while/body/eval_jaxpr/dot_general | solution.py:35
  211.0 4.0 %fusion.4 = f32[768,1024]{1,0:T(8,128)} fusion(bf16[768,384]{1,0:T(8,128)(2,1)} %copy-done.7, bf16[1,1024,384]{2,1,0:T(8,128)(2,1)} %param.11), kind=kOutput, calls=%fused_computation.22 | convolution fusion | flops 603979776 | bytes 4521984 | tf_op jit(solution)/shard_map/while/body/eval_jaxpr/dot_general | solution.py:30
  215.1 3.1 %add_convert_fusion = bf16[768,1024]{1,0:T(8,128)(2,1)S(1)} fusion(f32[768,1024]{1,0:T(8,128)} %fusion.4, bf16[768,384]{1,0:T(8,128)(2,1)} %get-tuple-element.65, bf16[1,1024,384]{2,1,0:T(8,128)(2,1)S(1)} %copy-done), kind=kOutput, calls=%fused_computation.9 | convolution fusion | flops 605552640 | bytes 6094848 | tf_op jit(solution)/shard_map/while/body/eval_jaxpr/dot_general | solution.py:31
  218.2 1.6 reshape.163
  219.8 14.2 %all-to-all-start.3 = ((bf16[128,6,1024]{2,1,0:T(8,128)(2,1)}), bf16[128,6,1024]{2,1,0:T(8,128)(2,1)}, u32[]{:S(2)}, u32[]{:S(2)}) async-start(bf16[128,6,1024]{2,1,0:T(8,128)(2,1)} %reshape.163), calls=%async_computation.3 | async-start | bytes 4194304 | tf_op jit(solution)/shard_map/all_to_all | solution.py:118
  234.1 0.3 reduce-scatter.8.cloned.1.call-start
  234.7 3.7 %fusion.2 = bf16[384,1024]{1,0:T(8,128)(2,1)} fusion(bf16[768,384]{1,0:T(8,128)(2,1)S(1)} %get-tuple-element.63, f32[768,1024]{1,0:T(8,128)} %reshape.168, f32[768]{0:T(1024)S(1)} %reshape.171), kind=kOutput, calls=%fused_computation.14 | convolution fusion | flops 605945856 | bytes 4525056 | tf_op jit(solution)/shard_map/while/body/eval_jaxpr/dot_general | solution.py:36
  238.7 3.5 %gather_fusion.4 = bf16[512]{0:T(512)(128)(2,1)S(1)} fusion(bf16[768]{0:T(1024)(128)(2,1)S(1)} %reshape.165, s32[1024]{0:T(1024)S(1)} %pad_clamp_fusion), kind=kCustom, calls=%fused_computation.4 | custom fusion | bytes 4096 | tf_op jit(solution)/shard_map/gather | solution.py:137
  242.4 0.7 copy.27
  243.0 1.7 bitcast_convert_fusion.2
  244.7 1.1 reduce-scatter.6.cloned.1.call-done
  245.9 1.7 bitcast_convert_fusion.1
  247.6 28.9 %reduce-scatter.8.cloned.1.call-done = bf16[384,256]{1,0:T(8,128)(2,1)} async-done(((bf16[384,1024]{1,0:T(8,128)(2,1)}), bf16[384,256]{1,0:T(8,128)(2,1)}) %reduce-scatter.8.cloned.1.call-update) | async-done | bytes 196624 | tf_op jit(solution)/shard_map/reduce_scatter | solution.py:145
  276.5 1.7 bitcast_convert_fusion
  278.2 6.8 %all-to-all-done.3 = bf16[128,6,1024]{2,1,0:T(8,128)(2,1)} async-done(((bf16[128,6,1024]{2,1,0:T(8,128)(2,1)}), bf16[128,6,1024]{2,1,0:T(8,128)(2,1)}, u32[]{:S(2)}, u32[]{:S(2)}) %all-to-all-start.3) | async-done | bytes 1572896 | tf_op jit(solution)/shard_map/all_to_all | solution.py:118
  285.0 2.6 reshape.164
  287.6 2.1 gather_fusion.3
  289.6 0.4 gather.27
  290.1 2.1 reduce_sum.35
  (50 shorter events, 2.4 us)
Async XLA Ops:
  7.2 180.5 %copy-start = (bf16[1,1024,384]{2,1,0:T(8,128)(2,1)S(1)}, bf16[1,1024,384]{2,1,0:T(8,128)(2,1)}, u32[]{:S(2)}) copy-start(bf16[1,1024,384]{2,1,0:T(8,128)(2,1)} %param.12) | copy-start | bytes 2359300
  10.5 27.2 %copy-start.1 = (bf16[128,1024]{1,0:T(8,128)(2,1)S(1)}, bf16[128,1024]{1,0:T(8,128)(2,1)}, u32[]{:S(2)}) copy-start(bf16[128,1024]{1,0:T(8,128)(2,1)} %param.7) | copy-start | bytes 786436
  19.1 36.0 %all-to-all-start = ((bf16[128,1,6]{2,1,0:T(2,128)(2,1)}), bf16[128,1,6]{2,1,0:T(2,128)(2,1)S(1)}, u32[]{:S(2)}, u32[]{:S(2)}) async-start(bf16[128,1,6]{2,1,0:T(2,128)(2,1)} %select_n.54), calls=%async_computation | async-start | bytes 131072 | tf_op jit(solution)/shard_map/all_to_all | solution.py:77
  41.3 2.5 copy-start.2
  120.1 60.2 %all-to-all-start.2 = ((bf16[128,6,1024]{2,1,0:T(8,128)(2,1)}), bf16[128,6,1024]{2,1,0:T(8,128)(2,1)}, u32[]{:S(2)}, u32[]{:S(2)}) async-start(bf16[128,6,1024]{2,1,0:T(8,128)(2,1)} %get-tuple-element.67), calls=%async_computation.2 | async-start | bytes 4194304 | tf_op jit(solution)/shard_map/all_to_all | solution.py:75
  129.3 113.7 %reduce-scatter.4.cloned.1.call-start = ((), (), s32[]{:S(2)}) async-start(), calls=%async_computation.8 | async-start | bytes 983040 | tf_op jit(solution)/shard_map/reduce_scatter | solution.py:139
  183.9 2.7 copy-start.5
  183.9 2.7 copy-start.6
  186.7 1.4 copy-start.3
  190.3 0.9 copy-start.7
  195.0 13.0 %copy-start.4 = (bf16[768,1024]{1,0:T(8,128)(2,1)S(1)}, bf16[768,1024]{1,0:T(8,128)(2,1)}, u32[]{:S(2)}) copy-start(bf16[768,1024]{1,0:T(8,128)(2,1)} %reshape.162) | copy-start | bytes 4718596
  199.1 20.7 %all-to-all-start.4 = ((bf16[128,1,6]{2,1,0:T(2,128)(2,1)}), bf16[128,1,6]{2,1,0:T(2,128)(2,1)S(1)}, u32[]{:S(2)}, u32[]{:S(2)}) async-start(bf16[128,1,6]{2,1,0:T(2,128)(2,1)} %convert_element_type.113), calls=%async_computation.4 | async-start | bytes 131072 | tf_op jit(solution)/shard_map/all_to_all | solution.py:125
  207.9 37.9 %reduce-scatter.6.cloned.1.call-start = ((), (), s32[]{:S(2)}) async-start(), calls=%async_computation.9 | async-start | bytes 983040 | tf_op jit(solution)/shard_map/reduce_scatter | solution.py:142
  219.8 65.1 %all-to-all-start.3 = ((bf16[128,6,1024]{2,1,0:T(8,128)(2,1)}), bf16[128,6,1024]{2,1,0:T(8,128)(2,1)}, u32[]{:S(2)}, u32[]{:S(2)}) async-start(bf16[128,6,1024]{2,1,0:T(8,128)(2,1)} %reshape.163), calls=%async_computation.3 | async-start | bytes 4194304 | tf_op jit(solution)/shard_map/all_to_all | solution.py:118
  234.1 42.4 %reduce-scatter.8.cloned.1.call-start = ((), (), s32[]{:S(2)}) async-start(), calls=%async_computation.10 | async-start | bytes 983040 | tf_op jit(solution)/shard_map/reduce_scatter | solution.py:145
Sparse Core Ops, SparseCore 0:
  193.2 22.0 reduce-scatter.3
  218.2 27.6 reduce-scatter.5
  248.7 27.7 reduce-scatter.7
where the time goes:
time: 302 us; the launch traced here: 299 us
  waiting for transfers between devices  82.1 us (27%)
  blocking collectives  65 us (22%)
  starting transfers between devices  51.2 us (17%)
  local copies, waits for them, and re-layouts  46.7 us (15%)
  matrix products  25 us (8%)
  other arithmetic  14.7 us (5%)
  between operations  14.1 us (5%)
    all_to_all x1, blocking collectives, shards(): lax.all_to_all(send_upstream, 'expert', split_axis=0, concat_axis=0, tile...  65 us
    all_to_all x1, waiting for transfers between devices, shards(): lax.all_to_all(send_inputs, 'expert', split_axis=0, concat_axis=0, tiled=...  45.2 us
    reduce_scatter x1, waiting for transfers between devices, shards(): lax.psum_scatter(grad_sums[2].astype(jnp.bfloat16), 'dp', scatter_dimensi...  28.9 us
    all_to_all x1, starting transfers between devices, shards(): lax.all_to_all(send_gates, 'expert', split_axis=0, concat_axis=0, tiled=T...  18.4 us
    all_to_all x1, starting transfers between devices, shards(): lax.all_to_all(route_grads.reshape(experts, most_rows, features), 'expert...  14.2 us
    gather x4, local copies, waits for them, and re-layouts, shards(): tokens.at[owner_token].get(mode='fill', fill_value=0)  13.4 us
    all_to_all x1, starting transfers between devices, shards(): lax.all_to_all(send_inputs, 'expert', split_axis=0, concat_axis=0, tiled=...  9.25 us
    all_to_all x1, starting transfers between devices, shards(): lax.all_to_all(gate_grads.reshape(experts, most_rows), 'expert', split_ax...  8.8 us
  transfers between devices with their start and end apart: 7, of which 4 were waited for; matrix products, arithmetic and copies ran while one was open for 18% of the time, Pallas kernels for 0%

commit v1 on v0

v1 whole, which is shorter than its diff:
```python
import functools

import jax
import jax.numpy as jnp
from jax import lax
from jax.experimental import pallas as pl
from jax.experimental.pallas import tpu as pltpu
from jax.sharding import PartitionSpec as P

F32, BF16 = jnp.float32, jnp.bfloat16
SLOTS = 6
BLOCK = 8
ROWS = 1024
CH = 256
VMEM = pl.BlockSpec(memory_space=pltpu.VMEM)


def dot(a, b, contract=((1,), (0,))):
    return lax.dot_general(a, b, (contract, ((), ())), preferred_element_type=F32)


def iota(shape, dim):
    return lax.broadcasted_iota(jnp.int32, shape, dim)


def one_hots(ids):
    experts = iota((128, 128), 0)
    named = jnp.zeros((128, 128), F32)
    for k in range(4):
        named = named + jnp.where(ids[k : k + 1, :] == experts, 1.0, 0.0)
    named = named.astype(BF16)
    earlier = jnp.where(iota((128, 128), 0) < iota((128, 128), 1), 1.0, 0.0).astype(BF16)
    rank = dot(named, earlier)
    rank = jnp.where(named.astype(F32) > 0.5, rank, -1.0).astype(BF16)
    spread = jnp.where(iota((ROWS, 128), 0) // BLOCK == iota((ROWS, 128), 1), 1.0, 0.0).astype(BF16)
    ranks = dot(spread, rank)
    place = (iota((ROWS, 128), 0) % BLOCK).astype(F32)
    main = jnp.where((ranks == place) & (place < 5.5), 1.0, 0.0)
    tails = [
        jnp.where((ranks == 3.0 * (place - 6.0) + j) & (place > 5.5), 1.0, 0.0) for j in range(3)
    ]
    return spread, main, tails


def pack_kernel(ids_ref, gate_ref, tok_ref, up_ref, out_ref):
    ids = ids_ref[...]
    spread, main, tails = one_hots(ids)
    gates = gate_ref[...].astype(F32)
    experts = iota((128, 128), 0)
    gate_of = jnp.zeros((128, 128), F32)
    for k in range(4):
        gate_of = gate_of + jnp.where(ids[k : k + 1, :] == experts, gates[k : k + 1, :], 0.0)
    gate_rows = dot(spread, gate_of.astype(BF16))
    for j in range(3):
        gate_col = jnp.sum((main + tails[j]) * gate_rows, axis=1, keepdims=True)
        pick = jnp.concatenate([main.astype(BF16), tails[j].astype(BF16)], axis=1)
        for which, ref in enumerate((tok_ref, up_ref)):
            both = jnp.concatenate(
                [ref[:, j * CH : (j + 1) * CH], ref[:, 3 * CH : 4 * CH]], axis=0
            )
            rows = dot(pick, both)
            if which == 1:
                rows = rows * gate_col
            base = which * 3 * CH + j * CH
            out_ref[:, :, base : base + CH] = rows.astype(BF16).reshape(128, BLOCK, CH)


def compute_kernel(
    got_ref, wg_ref, wu_ref, wd_ref, back_ref, gg_ref, gu_ref, gd_ref, x_s, s_s, dg_s, du_s, h_s
):
    row, col = iota((CH, CH), 0), iota((CH, CH), 1)
    same = row // BLOCK == col // BLOCK
    ra, ca = row % BLOCK, col % BLOCK
    unpack = jnp.concatenate(
        [
            jnp.where(same & (ra < 6) & (ca == 6 + ra // 3) & (ra % 3 == j), 1.0, 0.0)
            for j in range(3)
        ],
        axis=1,
    ).astype(BF16)
    repack = [
        jnp.where(same & (ra >= 6) & (ca == 3 * (ra - 6) + j), 1.0, 0.0).astype(BF16)
        for j in range(3)
    ]
    real = (iota((CH, 1), 0) % BLOCK) < SLOTS
    lane = iota((CH, 128), 1)

    def group(i, _):
        rows = pl.ds(pl.multiple_of(i * CH, CH), CH)
        srcs = pl.ds(pl.multiple_of(i * (CH // BLOCK), CH // BLOCK), CH // BLOCK)
        for which, ref in enumerate((x_s, s_s)):
            parts = []
            for j in range(3):
                base = which * 3 * CH + j * CH
                part = got_ref[srcs, :, base : base + CH].reshape(CH, CH)
                ref[rows, j * CH : (j + 1) * CH] = part
                parts.append(part)
            ref[rows, 3 * CH :] = dot(unpack, jnp.concatenate(parts, axis=0)).astype(BF16)
        x, s = x_s[rows, :], s_s[rows, :]
        pre_gate = dot(x, wg_ref[...])
        pre_up = dot(x, wu_ref[...])
        sig = jax.nn.sigmoid(pre_gate)
        silu = pre_gate * sig
        hidden = jnp.where(real, silu * pre_up, 0.0).astype(BF16)
        hgrad = dot(s, wd_ref[...], ((1,), (1,)))
        d_gate = jnp.where(
            real, hgrad * pre_up * sig * (1.0 + pre_gate * (1.0 - sig)), 0.0
        ).astype(BF16)
        d_up = jnp.where(real, hgrad * silu, 0.0).astype(BF16)
        h_s[rows, :] = hidden
        dg_s[rows, :] = d_gate
        du_s[rows, :] = d_up
        product = jnp.sum(hidden.astype(F32) * hgrad, axis=1, keepdims=True)
        back_ref[srcs, :, 3 * CH :] = (
            jnp.broadcast_to(product, (CH, 128)).astype(BF16).reshape(CH // BLOCK, BLOCK, 128)
        )
        tail = dot(d_gate, wg_ref[3 * CH :, :], ((1,), (1,))) + dot(
            d_up, wu_ref[3 * CH :, :], ((1,), (1,))
        )
        tail = tail.astype(BF16)
        for j in range(3):
            cols = slice(j * CH, (j + 1) * CH)
            part = dot(d_gate, wg_ref[cols, :], ((1,), (1,))) + dot(
                d_up, wu_ref[cols, :], ((1,), (1,))
            )
            part = part + dot(repack[j], tail)
            back_ref[srcs, :, cols] = part.astype(BF16).reshape(CH // BLOCK, BLOCK, CH)
        return 0

    lax.fori_loop(0, ROWS // CH, group, 0)

    def grads(i, _):
        cols = pl.ds(pl.multiple_of(i * CH, CH), CH)
        x = x_s[:, cols]
        gg_ref[cols, :] = dot(x, dg_s[...], ((0,), (0,))).astype(BF16)
        gu_ref[cols, :] = dot(x, du_s[...], ((0,), (0,))).astype(BF16)
        gd_ref[:, cols] = dot(h_s[...], s_s[:, cols], ((0,), (0,))).astype(BF16)
        return 0

    lax.fori_loop(0, 4, grads, 0)


def combine_kernel(ids_ref, gate_ref, back_ref, tok_ref, gate_out_ref):
    ids = ids_ref[...]
    spread, main, tails = one_hots(ids)
    main16 = main.astype(BF16)
    last = jnp.zeros((128, CH), F32)
    for j in range(3):
        part = back_ref[:, :, j * CH : (j + 1) * CH].reshape(ROWS, CH)
        tok_ref[:, j * CH : (j + 1) * CH] = dot(main16, part, ((0,), (0,))).astype(BF16)
        last = last + dot(tails[j].astype(BF16), part, ((0,), (0,)))
    tok_ref[:, 3 * CH :] = last.astype(BF16)
    product = back_ref[:, :, 3 * CH :].reshape(ROWS, 128)
    mine = dot(spread, (main * product.astype(F32)).astype(BF16), ((0,), (0,)))
    gates = gate_ref[...].astype(F32)
    experts = iota((128, 128), 0)
    for k in range(4):
        total = jnp.sum(jnp.where(ids[k : k + 1, :] == experts, mine, 0.0), axis=0, keepdims=True)
        gate_out_ref[k : k + 1, :] = (total / gates[k : k + 1, :]).astype(BF16)


def local(kernel, out_shape, args, scratch=(), name=None):
    return pl.pallas_call(
        kernel,
        out_shape=out_shape,
        in_specs=[VMEM] * len(args),
        out_specs=jax.tree.map(lambda _: VMEM, out_shape),
        scratch_shapes=scratch,
        compiler_params=pltpu.CompilerParams(vmem_limit_bytes=48 << 20),
        name=name,
    )(*args)


def shape(*dims, dtype=BF16):
    return jax.ShapeDtypeStruct(dims, dtype)


def shards(tokens, grad_out, expert_ids, gate_weight, w_gate, w_up, w_down):
    ids, gates = expert_ids.T, gate_weight.T
    send = local(pack_kernel, shape(128, BLOCK, 6 * CH), (ids, gates, tokens, grad_out), name="pack")
    got = lax.all_to_all(send, "expert", split_axis=0, concat_axis=0, tiled=True)
    back, part_gate, part_up, part_down = local(
        compute_kernel,
        (shape(128, BLOCK, 3 * CH + 128), shape(1024, 384), shape(1024, 384), shape(384, 1024)),
        (got, w_gate[0], w_up[0], w_down[0]),
        scratch=[
            pltpu.VMEM((ROWS, 1024), BF16),
            pltpu.VMEM((ROWS, 1024), BF16),
            pltpu.VMEM((ROWS, 384), BF16),
            pltpu.VMEM((ROWS, 384), BF16),
            pltpu.VMEM((ROWS, 384), BF16),
        ],
        name="compute",
    )
    home = lax.all_to_all(back, "expert", split_axis=0, concat_axis=0, tiled=True)
    grad_tokens, grad_gate = local(
        combine_kernel, (shape(128, 1024), shape(4, 128)), (ids, gates, home), name="combine"
    )
    sums = [
        lax.psum_scatter(part, "dp", scatter_dimension=dim, tiled=True).astype(F32)[None]
        for part, dim in ((part_gate, 0), (part_up, 0), (part_down, 1))
    ]
    return (grad_tokens, grad_gate.T, *sums)


def solution(mesh):
    rows = P(("dp", "expert"), None)
    weights = P("expert", None, None)
    return jax.shard_map(
        shards,
        mesh=mesh,
        in_specs=(rows, rows, rows, rows, weights, weights, weights),
        out_specs=(rows, rows, P("expert", "dp", None), P("expert", "dp", None), P("expert", None, "dp")),
        check_vma=False,
    )
```

time: 302 us -> 218 us (0.72)
  local copies, waits for them, and re-layouts: 46.7 us -> 3.28 us
  starting transfers between devices: 51.2 us -> 12.6 us
  blocking collectives: 65 us -> 91.1 us
  matrix products: 25 us -> 0 us
  Pallas kernels: 0 us -> 19.8 us
  waiting for transfers between devices: 82.1 us -> 70.6 us
  other arithmetic: 14.7 us -> 5.09 us
    all_to_all x4 -> x1, waiting for transfers between devices: 52 us -> 0.01 us  [shards(): lax.all_to_all(back, 'expert', split_axis=0, concat_axis=0, tiled=True)]
    reduce_scatter x3, waiting for transfers between devices: 30.1 us -> 69.2 us  [shards(): lax.psum_scatter(part, 'dp', scatter_dimension=dim, tiled=True).astype(F32)]
    all_to_all x4 -> x1, starting transfers between devices: 50.7 us -> 12.5 us  [shards(): lax.all_to_all(back, 'expert', split_axis=0, concat_axis=0, tiled=True)]
    all_to_all x1, blocking collectives: 65 us -> 91.1 us  [shards(): lax.all_to_all(send, 'expert', split_axis=0, concat_axis=0, tiled=True)]
    dot_general x9 -> x0, matrix products: 25 us -> none  [the longest x1 4.03 us: backward_tile(): lax.dot_general(d_gate, gate_matrix, across, preferred_element_type=jnp.f...]
    gather x8 -> x0, local copies, waits for them, and re-layouts: 24.4 us -> none  [the longest x4 13.4 us: shards(): tokens.at[owner_token].get(mode='fill', fill_value=0)]
    pallas_call x0 -> x3, Pallas kernels: none -> 19.8 us  [local(): pl.pallas_call(kernel, out_shape=out_shape, in_specs=[VMEM] * len(args),...]
    reshape x6 -> x0, local copies, waits for them, and re-layouts: 8.33 us -> none  [the longest x1 3.7 us: shards(): inputs = arrived_inputs.reshape(capacity, features)]
  transfers between devices with their start and end apart: 7 -> 4, of which waited for: 4 -> 3; matrix products, arithmetic and copies ran while one was open for 18% -> 2% of each run, Pallas kernels for 0% -> 0%
where the time goes in v1:
time: 218 us; the launch traced here: 216 us
  blocking collectives  91.1 us (42%)
  waiting for transfers between devices  70.6 us (32%)
  Pallas kernels  19.8 us (9%)
  between operations  13.8 us (6%)
  starting transfers between devices  12.6 us (6%)
  other arithmetic  5.09 us (2%)
  local copies, waits for them, and re-layouts  3.28 us (2%)
    all_to_all x1, blocking collectives, shards(): lax.all_to_all(send, 'expert', split_axis=0, concat_axis=0, tiled=True)  91.1 us
    reduce_scatter x3, waiting for transfers between devices, shards(): lax.psum_scatter(part, 'dp', scatter_dimension=dim, tiled=True).astype(F32)  69.2 us
    pallas_call x3, Pallas kernels, local(): pl.pallas_call(kernel, out_shape=out_shape, in_specs=[VMEM] * len(args),...  19.8 us
    all_to_all x1, starting transfers between devices, shards(): lax.all_to_all(back, 'expert', split_axis=0, concat_axis=0, tiled=True)  12.5 us
    broadcast_in_dim x3, other arithmetic, shards(): lax.psum_scatter(part, 'dp', scatter_dimension=dim, tiled=True).astype(F32)  5.09 us
  transfers between devices with their start and end apart: 4, of which 3 were waited for; matrix products, arithmetic and copies ran while one was open for 2% of the time, Pallas kernels for 0%

profile of v1, /device:TPU:1, one launch (start us, length us, event | category | flops | bytes accessed | tf_op | source)
XLA Modules:
  0.0 216.4 jit_solution(3161692981173692295)
XLA Ops:
  7.2 0.0 reduce-scatter.8.cloned.1.call-start
  7.2 0.0 copy-start.3
  7.2 0.9 copy-done.3
  8.2 0.0 copy-start.4
  8.2 0.9 copy-done.4
  9.1 0.0 copy-start.5
  9.1 0.7 copy-done.5
  9.8 0.0 copy-start.7
  9.8 0.7 copy-done.7
  10.5 1.5 pack.1
  11.9 0.0 copy-start
  11.9 0.0 copy-start.1
  12.0 0.0 copy-start.2
  12.0 91.1 %all_to_all.10.got_ref = bf16[128,8,1536]{2,1,0:T(8,128)(2,1)} all-to-all(bf16[128,8,1536]{2,1,0:T(8,128)(2,1)S(1)} %pack.1), channel_id=1, replica_groups=mesh['dp'=4,'expert'=128] {'expert'}, dimensions={0} | all-to-all | bytes 6291456 | tf_op jit(solution)/shard_map/all_to_all | solution.py:181
  103.1 0.0 copy-done
  103.1 0.0 copy-done.1
  103.1 0.0 copy-done.2
  103.1 16.2 %compute.1 = (bf16[128,8,896]{2,1,0:T(8,128)(2,1)}, bf16[1024,384]{1,0:T(8,128)(2,1)}, bf16[1024,384]{1,0:T(8,128)(2,1)}, bf16[384,1024]{1,0:T(8,128)(2,1)}) custom-call(bf16[128,8,1536]{2,1,0:T(8,128)(2,1)} %all_to_all.10.got_ref, bf16[1024,384]{1,0:T(8,128)(2,1)S(1)} %bitcast.15, bf16[1024,384]{1,0:T(8,128)(2,1)S(1)} %bitcast.16, ...), custom_call_target="tpu_custom_call" | custom-call | tf_op jit(solution)/shard_map/compute/pallas_call | solution.py:163
  119.3 0.0 reduce-scatter.8.cloned.1.call-update
  119.4 0.0 copy-start.6
  119.4 0.0 copy-start.8
  119.4 12.5 %all-to-all-start.1 = ((bf16[128,8,896]{2,1,0:T(8,128)(2,1)}), bf16[128,8,896]{2,1,0:T(8,128)(2,1)S(1)}, u32[]{:S(2)}, u32[]{:S(2)}) async-start(bf16[128,8,896]{2,1,0:T(8,128)(2,1)} %get-tuple-element.11), calls=%async_computation.1 | async-start | bytes 3670016 | tf_op jit(solution)/shard_map/all_to_all | solution.py:195
  131.8 0.0 reduce-scatter.6.cloned.1.call-start
  131.9 0.7 reduce-scatter.6.cloned.1.call-update
  132.6 0.0 reduce-scatter.4.cloned.1.call-start
  132.6 0.7 reduce-scatter.4.cloned.1.call-update
  133.3 11.7 %reduce-scatter.8.cloned.1.call-done = bf16[384,256]{1,0:T(8,128)(2,1)} async-done(((bf16[384,1024]{1,0:T(8,128)(2,1)}), bf16[384,256]{1,0:T(8,128)(2,1)}) %reduce-scatter.8.cloned.1.call-update) | async-done | bytes 196624 | tf_op jit(solution)/shard_map/reduce_scatter | solution.py:200
  145.1 1.7 bitcast_convert_fusion
  146.8 28.9 %reduce-scatter.6.cloned.1.call-done = bf16[256,384]{1,0:T(8,128)(2,1)} async-done(((bf16[1024,384]{1,0:T(8,128)(2,1)}), bf16[256,384]{1,0:T(8,128)(2,1)}) %reduce-scatter.6.cloned.1.call-update) | async-done | bytes 196624 | tf_op jit(solution)/shard_map/reduce_scatter | solution.py:200
  175.6 1.7 bitcast_convert_fusion.1
  177.3 28.7 %reduce-scatter.4.cloned.1.call-done = bf16[256,384]{1,0:T(8,128)(2,1)} async-done(((bf16[1024,384]{1,0:T(8,128)(2,1)}), bf16[256,384]{1,0:T(8,128)(2,1)}) %reduce-scatter.4.cloned.1.call-update) | async-done | bytes 196624 | tf_op jit(solution)/shard_map/reduce_scatter | solution.py:200
  206.0 1.7 bitcast_convert_fusion.2
  207.7 0.0 all-to-all-done.1.back_ref
  207.7 0.0 copy-done.6
  207.7 0.0 copy-done.8
  207.7 2.2 combine.1
Async XLA Ops:
  7.2 137.9 %reduce-scatter.8.cloned.1.call-start = ((), (), s32[]{:S(2)}) async-start(), calls=%async_computation.7 | async-start | bytes 983040 | tf_op jit(solution)/shard_map/reduce_scatter | solution.py:200
  7.2 1.0 copy-start.3
  8.2 0.9 copy-start.4
  9.1 0.7 copy-start.5
  9.8 0.7 copy-start.7
  11.9 91.2 %copy-start = (bf16[1,1024,384]{2,1,0:T(8,128)(2,1)S(1)}, bf16[1,1024,384]{2,1,0:T(8,128)(2,1)}, u32[]{:S(2)}) copy-start(bf16[1,1024,384]{2,1,0:T(8,128)(2,1)} %param.11) | copy-start | bytes 2359300
  11.9 91.1 %copy-start.1 = (bf16[1,1024,384]{2,1,0:T(8,128)(2,1)S(1)}, bf16[1,1024,384]{2,1,0:T(8,128)(2,1)}, u32[]{:S(2)}) copy-start(bf16[1,1024,384]{2,1,0:T(8,128)(2,1)} %param.12) | copy-start | bytes 2359300
  12.0 91.1 %copy-start.2 = (bf16[1,384,1024]{2,1,0:T(8,128)(2,1)S(1)}, bf16[1,384,1024]{2,1,0:T(8,128)(2,1)}, u32[]{:S(2)}) copy-start(bf16[1,384,1024]{2,1,0:T(8,128)(2,1)} %param.13) | copy-start | bytes 2359300
  119.4 88.3 %copy-start.6 = (s32[128,4]{0,1:T(4,128)S(1)}, s32[128,4]{0,1:T(4,128)}, u32[]{:S(2)}) copy-start(s32[128,4]{0,1:T(4,128)} %param.9) | copy-start | bytes 6148
  119.4 88.3 %copy-start.8 = (bf16[128,4]{0,1:T(4,128)(2,1)S(1)}, bf16[128,4]{0,1:T(4,128)(2,1)}, u32[]{:S(2)}) copy-start(bf16[128,4]{0,1:T(4,128)(2,1)} %param.10) | copy-start | bytes 3076
  119.4 88.3 %all-to-all-start.1 = ((bf16[128,8,896]{2,1,0:T(8,128)(2,1)}), bf16[128,8,896]{2,1,0:T(8,128)(2,1)S(1)}, u32[]{:S(2)}, u32[]{:S(2)}) async-start(bf16[128,8,896]{2,1,0:T(8,128)(2,1)} %get-tuple-element.11), calls=%async_computation.1 | async-start | bytes 3670016 | tf_op jit(solution)/shard_map/all_to_all | solution.py:195
  131.8 43.8 %reduce-scatter.6.cloned.1.call-start = ((), (), s32[]{:S(2)}) async-start(), calls=%async_computation.6 | async-start | bytes 983040 | tf_op jit(solution)/shard_map/reduce_scatter | solution.py:200
  132.6 73.4 %reduce-scatter.4.cloned.1.call-start = ((), (), s32[]{:S(2)}) async-start(), calls=%async_computation.5 | async-start | bytes 983040 | tf_op jit(solution)/shard_map/reduce_scatter | solution.py:200
Sparse Core Ops, SparseCore 0:
  119.5 25.5 reduce-scatter.7
  147.9 27.6 reduce-scatter.5
  178.5 27.4 reduce-scatter.3

commit v2 on v1

--- a/solution.py
+++ b/solution.py
@@ -31,20 +31,42 @@
     named = named.astype(BF16)
     earlier = jnp.where(iota((128, 128), 0) < iota((128, 128), 1), 1.0, 0.0).astype(BF16)
     rank = dot(named, earlier)
-    rank = jnp.where(named.astype(F32) > 0.5, rank, -1.0).astype(BF16)
+    rank = jnp.where(named.astype(F32) > 0.5, rank, -1.0)
     spread = jnp.where(iota((ROWS, 128), 0) // BLOCK == iota((ROWS, 128), 1), 1.0, 0.0).astype(BF16)
-    ranks = dot(spread, rank)
+    ranks = dot(spread, rank.astype(BF16))
     place = (iota((ROWS, 128), 0) % BLOCK).astype(F32)
     main = jnp.where((ranks == place) & (place < 5.5), 1.0, 0.0)
     tails = [
         jnp.where((ranks == 3.0 * (place - 6.0) + j) & (place > 5.5), 1.0, 0.0) for j in range(3)
     ]
-    return spread, main, tails
-
-
-def pack_kernel(ids_ref, gate_ref, tok_ref, up_ref, out_ref):
+    return rank, main, tails, spread
+
+
+def put_chunk(halves, blocks, j, rows):
+    low, high = halves
+    count = rows.shape[0] // BLOCK
+    if j == 0:
+        low[blocks, :, 0:256] = rows.reshape(count, BLOCK, CH)
+    elif j == 1:
+        low[blocks, :, 256:384] = rows[:, 0:128].reshape(count, BLOCK, 128)
+        high[blocks, :, 0:128] = rows[:, 128:256].reshape(count, BLOCK, 128)
+    else:
+        high[blocks, :, 128:384] = rows.reshape(count, BLOCK, CH)
+
+
+def get_chunk(halves, blocks, j):
+    low, high = halves
+    if j == 0:
+        return low[blocks, :, 0:256].reshape(-1, CH)
+    if j == 1:
+        left = low[blocks, :, 256:384].reshape(-1, 128)
+        return jnp.concatenate([left, high[blocks, :, 0:128].reshape(-1, 128)], axis=1)
+    return high[blocks, :, 128:384].reshape(-1, CH)
+
+
+def pack_kernel(ids_ref, gate_ref, tok_ref, up_ref, xa_ref, xb_ref, sa_ref, sb_ref):
     ids = ids_ref[...]
-    spread, main, tails = one_hots(ids)
+    _, main, tails, spread = one_hots(ids)
     gates = gate_ref[...].astype(F32)
     experts = iota((128, 128), 0)
     gate_of = jnp.zeros((128, 128), F32)
@@ -61,12 +83,13 @@
             rows = dot(pick, both)
             if which == 1:
                 rows = rows * gate_col
-            base = which * 3 * CH + j * CH
-            out_ref[:, :, base : base + CH] = rows.astype(BF16).reshape(128, BLOCK, CH)
+            halves = ((xa_ref, xb_ref), (sa_ref, sb_ref))[which]
+            put_chunk(halves, slice(None), j, rows.astype(BF16))
 
 
 def compute_kernel(
-    got_ref, wg_ref, wu_ref, wd_ref, back_ref, gg_ref, gu_ref, gd_ref, x_s, s_s, dg_s, du_s, h_s
+    xa_ref, xb_ref, sa_ref, sb_ref, wg_ref, wu_ref, wd_ref,
+    ba_ref, bb_ref, p_ref, gg_ref, gu_ref, gd_ref, x_s, s_s, dg_s, du_s, h_s
 ):
     row, col = iota((CH, CH), 0), iota((CH, CH), 1)
     same = row // BLOCK == col // BLOCK
@@ -91,8 +114,7 @@
         for which, ref in enumerate((x_s, s_s)):
             parts = []
             for j in range(3):
-                base = which * 3 * CH + j * CH
-                part = got_ref[srcs, :, base : base + CH].reshape(CH, CH)
+                part = get_chunk(((xa_ref, xb_ref), (sa_ref, sb_ref))[which], srcs, j)
                 ref[rows, j * CH : (j + 1) * CH] = part
                 parts.append(part)
             ref[rows, 3 * CH :] = dot(unpack, jnp.concatenate(parts, axis=0)).astype(BF16)
@@ -111,9 +133,8 @@
         dg_s[rows, :] = d_gate
         du_s[rows, :] = d_up
         product = jnp.sum(hidden.astype(F32) * hgrad, axis=1, keepdims=True)
-        back_ref[srcs, :, 3 * CH :] = (
-            jnp.broadcast_to(product, (CH, 128)).astype(BF16).reshape(CH // BLOCK, BLOCK, 128)
-        )
+        spots = jnp.where(lane == iota((CH, 128), 0) % BLOCK, product, 0.0)
+        p_ref[srcs, 0, :] = jnp.sum(spots.reshape(CH // BLOCK, BLOCK, 128), axis=1)
         tail = dot(d_gate, wg_ref[3 * CH :, :], ((1,), (1,))) + dot(
             d_up, wu_ref[3 * CH :, :], ((1,), (1,))
         )
@@ -124,7 +145,7 @@
                 d_up, wu_ref[cols, :], ((1,), (1,))
             )
             part = part + dot(repack[j], tail)
-            back_ref[srcs, :, cols] = part.astype(BF16).reshape(CH // BLOCK, BLOCK, CH)
+            put_chunk((ba_ref, bb_ref), srcs, j, part.astype(BF16))
         return 0
 
     lax.fori_loop(0, ROWS // CH, group, 0)
@@ -132,31 +153,209 @@
     def grads(i, _):
         cols = pl.ds(pl.multiple_of(i * CH, CH), CH)
         x = x_s[:, cols]
-        gg_ref[cols, :] = dot(x, dg_s[...], ((0,), (0,))).astype(BF16)
-        gu_ref[cols, :] = dot(x, du_s[...], ((0,), (0,))).astype(BF16)
-        gd_ref[:, cols] = dot(h_s[...], s_s[:, cols], ((0,), (0,))).astype(BF16)
+        gg_ref[i] = dot(x, dg_s[...], ((0,), (0,))).astype(BF16)
+        gu_ref[i] = dot(x, du_s[...], ((0,), (0,))).astype(BF16)
+        gd_ref[i] = dot(h_s[...], s_s[:, cols], ((0,), (0,))).astype(BF16)
         return 0
 
     lax.fori_loop(0, 4, grads, 0)
 
 
-def combine_kernel(ids_ref, gate_ref, back_ref, tok_ref, gate_out_ref):
+def combine_kernel(
+    ids_ref, gate_ref, ba_ref, bb_ref, p_ref, rg_ref, ru_ref, rd_ref,
+    tok_ref, gate_out_ref, gg_ref, gu_ref, gd_ref
+):
+    for part, total in ((rg_ref, gg_ref), (ru_ref, gu_ref), (rd_ref, gd_ref)):
+        total[0] = sum(part[i].astype(F32) for i in range(1, 4)) + part[0].astype(F32)
     ids = ids_ref[...]
-    spread, main, tails = one_hots(ids)
-    main16 = main.astype(BF16)
+    rank, main, tails, _ = one_hots(ids)
+    main = main.astype(BF16)
     last = jnp.zeros((128, CH), F32)
     for j in range(3):
-        part = back_ref[:, :, j * CH : (j + 1) * CH].reshape(ROWS, CH)
-        tok_ref[:, j * CH : (j + 1) * CH] = dot(main16, part, ((0,), (0,))).astype(BF16)
+        part = get_chunk((ba_ref, bb_ref), slice(None), j)
+        tok_ref[:, j * CH : (j + 1) * CH] = dot(main, part, ((0,), (0,))).astype(BF16)
         last = last + dot(tails[j].astype(BF16), part, ((0,), (0,)))
     tok_ref[:, 3 * CH :] = last.astype(BF16)
-    product = back_ref[:, :, 3 * CH :].reshape(ROWS, 128)
-    mine = dot(spread, (main * product.astype(F32)).astype(BF16), ((0,), (0,)))
+    mine = jnp.zeros((128, 128), F32)
+    for r in range(SLOTS):
+        mine = mine + jnp.where(rank == r, p_ref[:, 0, r : r + 1], 0.0)
     gates = gate_ref[...].astype(F32)
     experts = iota((128, 128), 0)
     for k in range(4):
         total = jnp.sum(jnp.where(ids[k : k + 1, :] == experts, mine, 0.0), axis=0, keepdims=True)
         gate_out_ref[k : k + 1, :] = (total / gates[k : k + 1, :]).astype(BF16)
+
+
+def ring_step(i):
+    return jnp.where(i % 2 == 1, (i + 1) // 2, 8 - i // 2)
+
+
+class Exchange:
+    def __init__(self, route, src, mid, dst, send1, recv1, send2, recv2):
+        self.route, self.src, self.mid, self.dst = route, src, mid, dst
+        self.send1, self.recv1, self.send2, self.recv2 = send1, recv1, send2, recv2
+        self.dp, me = lax.axis_index("dp"), lax.axis_index("expert")
+        self.z, self.y, self.c = me // 16, (me // 2) % 8, me % 2
+
+    def slab(self, p):
+        return self.src.at[p] if self.route == "z" else self.src.at[:, p]
+
+    def landing(self):
+        return self.dst.at[:, self.y, self.c] if self.route == "z" else self.dst.at[self.z, :, self.c]
+
+    def peer(self, p, c):
+        return p * 16 + self.y * 2 + c, self.z * 16 + p * 2 + c
+
+    def copy1(self, i):
+        along = self.z if self.route == "z" else self.y
+        p = (along + ring_step(i)) % 8
+        by_z, by_y = self.peer(p, self.c)
+        return pltpu.make_async_remote_copy(
+            src_ref=self.slab(p),
+            dst_ref=self.mid.at[along],
+            send_sem=self.send1.at[i],
+            recv_sem=self.recv1,
+            device_id=(self.dp, by_z if self.route == "z" else by_y),
+            device_id_type=pl.DeviceIdType.MESH,
+        )
+
+    def copy2(self, i):
+        across = self.y if self.route == "z" else self.z
+        p = (across + jnp.where(i < 14, ring_step(i // 2 + 1), 0)) % 8
+        c = jnp.where(i < 14, i % 2, 1 - self.c)
+        by_z, by_y = self.peer(p, c)
+        return pltpu.make_async_remote_copy(
+            src_ref=self.mid.at[:, p, c],
+            dst_ref=self.landing(),
+            send_sem=self.send2.at[i],
+            recv_sem=self.recv2,
+            device_id=(self.dp, by_y if self.route == "z" else by_z),
+            device_id_type=pl.DeviceIdType.MESH,
+        )
+
+    def phase1(self):
+        def one(i, _):
+            self.copy1(i).start()
+            return 0
+
+        lax.fori_loop(1, 8, one, 0)
+        along = self.z if self.route == "z" else self.y
+        pltpu.make_async_copy(self.slab(along), self.mid.at[along], self.recv1).start()
+
+    def phase2(self):
+        pltpu.make_async_copy(self.mid, self.mid, self.recv1).wait()
+
+        def one(i, _):
+            self.copy2(i).start()
+            return 0
+
+        lax.fori_loop(0, 15, one, 0)
+        across = self.y if self.route == "z" else self.z
+        pltpu.make_async_copy(self.mid.at[:, across, self.c], self.landing(), self.recv2).start()
+
+    def arrived(self):
+        pltpu.make_async_copy(self.dst, self.dst, self.recv2).wait()
+
+    def sent(self):
+        def one(i, _):
+            self.copy1(i).wait_send()
+            return 0
+
+        lax.fori_loop(1, 8, one, 0)
+
+        def two(i, _):
+            self.copy2(i).wait_send()
+            return 0
+
+        lax.fori_loop(0, 15, two, 0)
+
+
+def greet(with_dp):
+    dp, me = lax.axis_index("dp"), lax.axis_index("expert")
+    z, y, c = me // 16, (me // 2) % 8, me % 2
+    barrier = pltpu.get_barrier_semaphore()
+
+    def signal(i, target):
+        pl.semaphore_signal(barrier, inc=1, device_id=target, device_id_type=pl.DeviceIdType.MESH)
+
+    def rings(i, _):
+        for core in (c, 1 - c):
+            signal(i, (dp, ((z + i) % 8) * 16 + y * 2 + core))
+            signal(i, (dp, z * 16 + ((y + i) % 8) * 2 + core))
+        return 0
+
+    lax.fori_loop(1, 8, rings, 0)
+    signal(0, (dp, z * 16 + y * 2 + 1 - c))
+    if with_dp:
+        for i in range(1, 4):
+            signal(i, ((dp + i) % 4, me))
+    pl.semaphore_wait(barrier, 32 if with_dp else 29)
+
+
+def exchange_kernel(routes, scatter, *refs):
+    n = len(routes)
+    refs = list(refs)
+    take = lambda count: [refs.pop(0) for _ in range(count)]
+    srcs, parts = take(n), take(scatter)
+    dsts, lands = take(n), take(scatter)
+    mids = take(n)
+    send1, recv1, send2, recv2, send3, recv3 = take(6)
+    dp, me = lax.axis_index("dp"), lax.axis_index("expert")
+    greet(scatter > 0)
+    streams = [
+        Exchange(
+            routes[i], srcs[i], mids[i], dsts[i], send1.at[i], recv1.at[i], send2.at[i], recv2.at[i]
+        )
+        for i in range(n)
+    ]
+    for stream in streams:
+        stream.phase1()
+
+    def scatter_copy(k, i):
+        target = (dp + i) % 4
+        return pltpu.make_async_remote_copy(
+            src_ref=parts[k].at[target],
+            dst_ref=lands[k].at[dp],
+            send_sem=send3.at[k, i],
+            recv_sem=recv3.at[k],
+            device_id=(target, me),
+            device_id_type=pl.DeviceIdType.MESH,
+        )
+
+    for k in range(scatter):
+        for i in (1, 3, 2):
+            scatter_copy(k, i).start()
+        pltpu.make_async_copy(parts[k].at[dp], lands[k].at[dp], recv3.at[k]).start()
+    for stream in streams:
+        stream.phase2()
+    for stream in streams:
+        stream.arrived()
+    for stream in streams:
+        stream.sent()
+    for k in range(scatter):
+        pltpu.make_async_copy(lands[k], lands[k], recv3.at[k]).wait()
+        for i in (1, 3, 2):
+            scatter_copy(k, i).wait_send()
+
+
+def exchange(routes, arrays, parts, collective_id, name):
+    n = len(arrays)
+    wide = [a.reshape(8, 8, 2, *a.shape[1:]) for a in arrays]
+    like = [jax.ShapeDtypeStruct(a.shape, a.dtype) for a in wide + list(parts)]
+    sem = pltpu.SemaphoreType.DMA
+    outs = pl.pallas_call(
+        functools.partial(exchange_kernel, routes, len(parts)),
+        out_shape=like,
+        in_specs=[VMEM] * len(like),
+        out_specs=[VMEM] * len(like),
+        scratch_shapes=[pltpu.VMEM(a.shape, a.dtype) for a in wide]
+        + [sem((n, 8)), sem((n,)), sem((n, 16)), sem((n,)), sem((3, 4)), sem((3,))],
+        compiler_params=pltpu.CompilerParams(
+            collective_id=collective_id, has_side_effects=True, vmem_limit_bytes=24 << 20
+        ),
+        name=name,
+    )(*wide, *parts)
+    return [o.reshape(128, *o.shape[3:]) for o in outs[:n]], outs[n:]
 
 
 def local(kernel, out_shape, args, scratch=(), name=None):
@@ -177,12 +376,14 @@
 
 def shards(tokens, grad_out, expert_ids, gate_weight, w_gate, w_up, w_down):
     ids, gates = expert_ids.T, gate_weight.T
-    send = local(pack_kernel, shape(128, BLOCK, 6 * CH), (ids, gates, tokens, grad_out), name="pack")
-    got = lax.all_to_all(send, "expert", split_axis=0, concat_axis=0, tiled=True)
-    back, part_gate, part_up, part_down = local(
+    half = shape(128, BLOCK, 384)
+    send = local(pack_kernel, (half,) * 4, (ids, gates, tokens, grad_out), name="pack")
+    got, _ = exchange(("z", "y", "z", "y"), send, [], 0, "dispatch")
+    *back, part_gate, part_up, part_down = local(
         compute_kernel,
-        (shape(128, BLOCK, 3 * CH + 128), shape(1024, 384), shape(1024, 384), shape(384, 1024)),
-        (got, w_gate[0], w_up[0], w_down[0]),
+        (half, half, shape(128, 1, 128, dtype=F32))
+        + (shape(4, 256, 384), shape(4, 256, 384), shape(4, 384, 256)),
+        (*got, w_gate[0], w_up[0], w_down[0]),
         scratch=[
             pltpu.VMEM((ROWS, 1024), BF16),
             pltpu.VMEM((ROWS, 1024), BF16),
@@ -192,15 +393,15 @@
         ],
         name="compute",
     )
-    home = lax.all_to_all(back, "expert", split_axis=0, concat_axis=0, tiled=True)
-    grad_tokens, grad_gate = local(
-        combine_kernel, (shape(128, 1024), shape(4, 128)), (ids, gates, home), name="combine"
+    home, sums = exchange(("z", "y", "z"), back, [part_gate, part_up, part_down], 1, "return")
+    wide = shape(1, 256, 384, dtype=F32)
+    grad_tokens, grad_gate, *grads = local(
+        combine_kernel,
+        (shape(128, 1024), shape(4, 128), wide, wide, shape(1, 384, 256, dtype=F32)),
+        (ids, gates, *home, *sums),
+        name="combine",
     )
-    sums = [
-        lax.psum_scatter(part, "dp", scatter_dimension=dim, tiled=True).astype(F32)[None]
-        for part, dim in ((part_gate, 0), (part_up, 0), (part_down, 1))
-    ]
-    return (grad_tokens, grad_gate.T, *sums)
+    return (grad_tokens, grad_gate.T, *grads)
 
 
 def solution(mesh):

time: 218 us -> 157 us (0.72)
  Pallas kernels: 19.8 us -> 151 us
  blocking collectives: 91.1 us -> 0 us
  waiting for transfers between devices: 70.6 us -> 0 us
  between operations: 13.8 us -> 0.68 us
  starting transfers between devices: 12.6 us -> 0 us
  other arithmetic: 5.09 us -> 0 us
    pallas_call x0 -> x2, Pallas kernels: none -> 131 us  [exchange(): pl.pallas_call(functools.partial(exchange_kernel, routes, len(parts)), ou...]
    all_to_all x1 -> x0, blocking collectives: 91.1 us -> none  [shards(): lax.all_to_all(send, 'expert', split_axis=0, concat_axis=0, tiled=True)]
    reduce_scatter x3 -> x0, waiting for transfers between devices: 69.2 us -> none  [shards(): lax.psum_scatter(part, 'dp', scatter_dimension=dim, tiled=True).astype(F32)]
    all_to_all x1 -> x0, starting transfers between devices: 12.5 us -> none  [shards(): lax.all_to_all(back, 'expert', split_axis=0, concat_axis=0, tiled=True)]
    broadcast_in_dim x3 -> x0, other arithmetic: 5.09 us -> none  [shards(): lax.psum_scatter(part, 'dp', scatter_dimension=dim, tiled=True).astype(F32)]
    unnamed x18 -> x12, local copies, waits for them, and re-layouts: 3.28 us -> 4.37 us
  transfers between devices with their start and end apart: 4 -> 0, of which waited for: 3 -> 0; matrix products, arithmetic and copies ran while one was open for 2% -> 0% of each run, Pallas kernels for 0% -> 0%
where the time goes in v2:
time: 157 us; the launch traced here: 156 us
  Pallas kernels  151 us (96%)
  local copies, waits for them, and re-layouts  4.37 us (3%)
    pallas_call x2, Pallas kernels, exchange(): pl.pallas_call(functools.partial(exchange_kernel, routes, len(parts)), ou...  131 us
    pallas_call x3, Pallas kernels, local(): pl.pallas_call(kernel, out_shape=out_shape, in_specs=[VMEM] * len(args),...  19.4 us
    unnamed x12, local copies, waits for them, and re-layouts  4.37 us

profile of v2, /device:TPU:1, one launch (start us, length us, event | category | flops | bytes accessed | tf_op | source)
XLA Modules:
  0.0 155.8 jit_solution(3892480159851346245)
XLA Ops:
  0.6 0.0 copy-start.4
  0.6 0.0 copy-start.5
  0.7 0.7 copy-done.4
  1.3 0.0 copy-done.5
  1.3 0.0 copy-start.2
  1.3 0.9 copy-done.2
  2.3 0.0 copy-start.3
  2.3 0.9 copy-done.3
  3.2 1.5 pack.1
  4.7 86.7 %dispatch.1 = (bf16[8,8,2,8,384]{4,3,2,1,0:T(8,128)(2,1)S(1)}, bf16[8,8,2,8,384]{4,3,2,1,0:T(8,128)(2,1)S(1)}, bf16[8,8,2,8,384]{4,3,2,1,0:T(8,128)(2,1)S(1)}, bf16[8,8,2,8,384]{4,3,2,1,0:T(8,128)(2,1)S(1)}) custom-call(bf16[8,8,2,8,384]{4,3,2,1,0:T(8,128)(2,1)S(1)} %bitcast.20, bf16[8,8,2,8,384]{4,3,2,1,0:T(8,128)(2,1)S(1)} %bitcast.21, ...), custom_call_target="tpu_custom_call" | custom-call | tf_op jit(solution)/shard_map/dispatch/pallas_call | solution.py:346
  91.4 0.0 copy-start
  91.4 0.9 copy-done
  92.2 0.0 copy-start.1
  92.2 0.9 copy-done.1
  93.2 15.2 %compute.1 = (bf16[128,8,384]{2,1,0:T(8,128)(2,1)S(1)}, bf16[128,8,384]{2,1,0:T(8,128)(2,1)S(1)}, f32[128,1,128]{2,1,0:T(1,128)S(1)}, bf16[4,256,384]{2,1,0:T(8,...) custom-call(bf16[128,8,384]{2,1,0:T(8,128)(2,1)S(1)} %bitcast.28, ...), custom_call_target="tpu_custom_call" | custom-call | tf_op jit(solution)/shard_map/compute/pallas_call | solution.py:362
  108.4 44.7 %return.1 = (bf16[8,8,2,8,384]{4,3,2,1,0:T(8,128)(2,1)S(1)}, bf16[8,8,2,8,384]{4,3,2,1,0:T(8,128)(2,1)S(1)}, f32[8,8,2,1,128]{4,3,2,1,0:T(1,128)S(1)}, bf16[4,25...) custom-call(bf16[8,8,2,8,384]{4,3,2,1,0:T(8,128)(2,1)S(1)} %bitcast.26, ...), custom_call_target="tpu_custom_call" | custom-call | tf_op jit(solution)/shard_map/return/pallas_call | solution.py:346
  153.1 2.8 %combine.1 = (bf16[128,1024]{1,0:T(8,128)(2,1)}, bf16[4,128]{1,0:T(4,128)(2,1)}, f32[1,256,384]{2,1,0:T(8,128)}, f32[1,256,384]{2,1,0:T(8,128)}, f32[1,384,256]{2,1,0:T(8,128)}) custom-call(s32[4,128]{1,0:T(4,128)S(1)} %bitcast.35, bf16[4,128]{1,0:T(4,128)(2,1)S(1)} %bitcast.37, bf16[128,8,384]{2,1,0:T(8,128)(2,1)S(1)} %bitcast.24, ...), custom_call_target="tpu_custom_call" | custom-call | tf_op jit(solution)/shard_map/combine/pallas_call | solution.py:362
Async XLA Ops:
  0.6 0.7 copy-start.4
  0.6 0.7 copy-start.5
  1.3 0.9 copy-start.2
  2.3 0.9 copy-start.3
  91.4 0.9 copy-start
  92.2 0.9 copy-start.1

commit v3 on v2

v3 whole, which is shorter than its diff:
```python
import functools

import jax
import jax.numpy as jnp
from jax import lax
from jax.experimental import pallas as pl
from jax.experimental.pallas import tpu as pltpu
from jax.sharding import PartitionSpec as P

F32, BF16 = jnp.float32, jnp.bfloat16
SLOTS = 6
BLOCK = 8
ROWS = 1024
CH = 256
VMEM = pl.BlockSpec(memory_space=pltpu.VMEM)


def dot(a, b, contract=((1,), (0,))):
    return lax.dot_general(a, b, (contract, ((), ())), preferred_element_type=F32)


def iota(shape, dim):
    return lax.broadcasted_iota(jnp.int32, shape, dim)


def one_hots(ids):
    experts = iota((128, 128), 0)
    named = jnp.zeros((128, 128), F32)
    for k in range(4):
        named = named + jnp.where(ids[k : k + 1, :] == experts, 1.0, 0.0)
    named = named.astype(BF16)
    earlier = jnp.where(iota((128, 128), 0) < iota((128, 128), 1), 1.0, 0.0).astype(BF16)
    rank = dot(named, earlier)
    rank = jnp.where(named.astype(F32) > 0.5, rank, -1.0)
    spread = jnp.where(iota((ROWS, 128), 0) // BLOCK == iota((ROWS, 128), 1), 1.0, 0.0).astype(BF16)
    ranks = dot(spread, rank.astype(BF16))
    place = (iota((ROWS, 128), 0) % BLOCK).astype(F32)
    main = jnp.where((ranks == place) & (place < 5.5), 1.0, 0.0)
    tails = [
        jnp.where((ranks == 3.0 * (place - 6.0) + j) & (place > 5.5), 1.0, 0.0) for j in range(3)
    ]
    return rank, main, tails, spread


def put_chunk(halves, blocks, j, rows):
    low, high = halves
    lead = low.at[blocks].shape[:-1]

    def put(ref, at, value):
        ref[(blocks, *[slice(None)] * (len(lead) - 1), at)] = value.reshape(*lead, value.shape[1])

    if j == 0:
        put(low, slice(0, 256), rows)
    elif j == 1:
        put(low, slice(256, 384), rows[:, 0:128])
        put(high, slice(0, 128), rows[:, 128:256])
    else:
        put(high, slice(128, 384), rows)


def get_chunk(halves, blocks, j):
    low, high = halves

    def get(ref, lo, hi):
        at = (blocks, *[slice(None)] * (len(ref.shape) - 2), slice(lo, hi))
        return ref[at].reshape(-1, hi - lo)

    if j == 0:
        return get(low, 0, 256)
    if j == 1:
        return jnp.concatenate([get(low, 256, 384), get(high, 0, 128)], axis=1)
    return get(high, 128, 384)


def pack_kernel(ids_ref, gate_ref, tok_ref, up_ref, xa_ref, xb_ref, sa_ref, sb_ref):
    ids = ids_ref[...]
    _, main, tails, spread = one_hots(ids)
    gates = gate_ref[...].astype(F32)
    experts = iota((128, 128), 0)
    gate_of = jnp.zeros((128, 128), F32)
    for k in range(4):
        gate_of = gate_of + jnp.where(ids[k : k + 1, :] == experts, gates[k : k + 1, :], 0.0)
    gate_rows = dot(spread, gate_of.astype(BF16))
    for j in range(3):
        gate_col = jnp.sum((main + tails[j]) * gate_rows, axis=1, keepdims=True)
        pick = jnp.concatenate([main.astype(BF16), tails[j].astype(BF16)], axis=1)
        for which, ref in enumerate((tok_ref, up_ref)):
            both = jnp.concatenate(
                [ref[:, j * CH : (j + 1) * CH], ref[:, 3 * CH : 4 * CH]], axis=0
            )
            rows = dot(pick, both)
            if which == 1:
                rows = rows * gate_col
            halves = ((xa_ref, xb_ref), (sa_ref, sb_ref))[which]
            put_chunk(halves, slice(None), j, rows.astype(BF16))


def combine_kernel(
    ids_ref, gate_ref, ba_ref, bb_ref, p_ref, rg_ref, ru_ref, rd_ref,
    tok_ref, gate_out_ref, gg_ref, gu_ref, gd_ref
):
    for part, total in ((rg_ref, gg_ref), (ru_ref, gu_ref), (rd_ref, gd_ref)):
        total[0] = sum(part[i].astype(F32) for i in range(1, 4)) + part[0].astype(F32)
    ids = ids_ref[...]
    rank, main, tails, _ = one_hots(ids)
    main = main.astype(BF16)
    last = jnp.zeros((128, CH), F32)
    for j in range(3):
        part = get_chunk((ba_ref, bb_ref), slice(None), j)
        tok_ref[:, j * CH : (j + 1) * CH] = dot(main, part, ((0,), (0,))).astype(BF16)
        last = last + dot(tails[j].astype(BF16), part, ((0,), (0,)))
    tok_ref[:, 3 * CH :] = last.astype(BF16)
    mine = jnp.zeros((128, 128), F32)
    for r in range(SLOTS):
        mine = mine + jnp.where(rank == r, p_ref[:, 0, r : r + 1], 0.0)
    gates = gate_ref[...].astype(F32)
    experts = iota((128, 128), 0)
    for k in range(4):
        total = jnp.sum(jnp.where(ids[k : k + 1, :] == experts, mine, 0.0), axis=0, keepdims=True)
        gate_out_ref[k : k + 1, :] = (total / gates[k : k + 1, :]).astype(BF16)


def ring_step(i):
    return jnp.where(i % 2 == 1, (i + 1) // 2, 8 - i // 2)


class Exchange:
    def __init__(self, route, src, mid, dst, send1, recv1, send2, recv2):
        self.route, self.src, self.mid, self.dst = route, src, mid, dst
        self.send1, self.recv1, self.send2, self.recv2 = send1, recv1, send2, recv2
        self.dp, me = lax.axis_index("dp"), lax.axis_index("expert")
        self.z, self.y, self.c = me // 16, (me // 2) % 8, me % 2

    def slab(self, p):
        return self.src.at[p] if self.route == "z" else self.src.at[:, p]

    def landing(self):
        return self.dst.at[:, self.y, self.c] if self.route == "z" else self.dst.at[self.z, :, self.c]

    def peer(self, p, c):
        return p * 16 + self.y * 2 + c, self.z * 16 + p * 2 + c

    def along(self):
        return self.z if self.route == "z" else self.y

    def first(self, p):
        by_z, by_y = self.peer(p, self.c)
        return by_z if self.route == "z" else by_y

    def copy1(self, p):
        return pltpu.make_async_remote_copy(
            src_ref=self.slab(p),
            dst_ref=self.mid.at[self.along()],
            send_sem=self.send1.at[p],
            recv_sem=self.recv1,
            device_id=(self.dp, self.first(p)),
            device_id_type=pl.DeviceIdType.MESH,
        )

    def piece1(self, p, g):
        zs = pl.ds(2 * g, 2)
        return pltpu.make_async_remote_copy(
            src_ref=self.src.at[zs, p],
            dst_ref=self.mid.at[self.y, zs],
            send_sem=self.send1.at[8 * g + p],
            recv_sem=self.recv1,
            device_id=(self.dp, self.first(p)),
            device_id_type=pl.DeviceIdType.MESH,
        )

    def group1(self, g):
        if self.route == "z":
            for p in (2 * g, 2 * g + 1):

                @pl.when(p != self.z)
                def _():
                    self.copy1(p).start()

                @pl.when(p == self.z)
                def _():
                    pltpu.make_async_copy(self.slab(p), self.mid.at[p], self.recv1).start()

        else:

            def one(i, _):
                self.piece1((self.y + ring_step(i)) % 8, g).start()
                return 0

            lax.fori_loop(1, 8, one, 0)
            zs = pl.ds(2 * g, 2)
            pltpu.make_async_copy(
                self.src.at[zs, self.y], self.mid.at[self.y, zs], self.recv1
            ).start()

    def copy2(self, i):
        across = self.y if self.route == "z" else self.z
        p = (across + jnp.where(i < 14, ring_step(i // 2 + 1), 0)) % 8
        c = jnp.where(i < 14, i % 2, 1 - self.c)
        by_z, by_y = self.peer(p, c)
        return pltpu.make_async_remote_copy(
            src_ref=self.mid.at[:, p, c],
            dst_ref=self.landing(),
            send_sem=self.send2.at[i],
            recv_sem=self.recv2,
            device_id=(self.dp, by_y if self.route == "z" else by_z),
            device_id_type=pl.DeviceIdType.MESH,
        )

    def phase1(self):
        along = self.along()

        def one(i, _):
            self.copy1((along + ring_step(i)) % 8).start()
            return 0

        lax.fori_loop(1, 8, one, 0)
        pltpu.make_async_copy(self.slab(along), self.mid.at[along], self.recv1).start()

    def phase2(self):
        pltpu.make_async_copy(self.mid, self.mid, self.recv1).wait()

        def one(i, _):
            self.copy2(i).start()
            return 0

        lax.fori_loop(0, 15, one, 0)
        across = self.y if self.route == "z" else self.z
        pltpu.make_async_copy(self.mid.at[:, across, self.c], self.landing(), self.recv2).start()

    def arrived(self):
        pltpu.make_async_copy(self.dst, self.dst, self.recv2).wait()

    def sent(self, grouped=False):
        def one(i, _):
            p = (self.along() + i) % 8
            if grouped and self.route == "y":
                for g in range(4):
                    self.piece1(p, g).wait_send()
            else:
                self.copy1(p).wait_send()
            return 0

        lax.fori_loop(1, 8, one, 0)

        def two(i, _):
            self.copy2(i).wait_send()
            return 0

        lax.fori_loop(0, 15, two, 0)


def greet():
    dp, me = lax.axis_index("dp"), lax.axis_index("expert")
    z, y, c = me // 16, (me // 2) % 8, me % 2
    barrier = pltpu.get_barrier_semaphore()

    def signal(target):
        pl.semaphore_signal(barrier, inc=1, device_id=target, device_id_type=pl.DeviceIdType.MESH)

    def rings(i, _):
        for core in (c, 1 - c):
            signal((dp, ((z + i) % 8) * 16 + y * 2 + core))
            signal((dp, z * 16 + ((y + i) % 8) * 2 + core))
        return 0

    lax.fori_loop(1, 8, rings, 0)
    signal((dp, z * 16 + y * 2 + 1 - c))
    for i in range(1, 4):
        signal(((dp + i) % 4, me))
    pl.semaphore_wait(barrier, 32)


def main_kernel(*refs):
    refs = list(refs)
    take = lambda count: [refs.pop(0) for _ in range(count)]
    sends, weights_hbm = take(4), take(3)
    homes, lands = take(3), take(3)
    mids, gots, weights = take(4), take(4), take(3)
    x_s, s_s, a_s, silu_s, dg_s, du_s, h_s = take(7)
    backs, back_mids, parts = take(3), take(3), take(3)
    send1, recv1, send2, recv2, send3, recv3, load = take(7)
    dp, me = lax.axis_index("dp"), lax.axis_index("expert")
    loads = [pltpu.make_async_copy(weights_hbm[i], weights[i], load.at[i]) for i in range(3)]
    for one in loads:
        one.start()
    greet()
    outward = [
        Exchange(
            "zyzy"[i], sends[i], mids[i], gots[i], send1.at[i], recv1.at[i], send2.at[i], recv2.at[i]
        )
        for i in range(4)
    ]
    homeward = [
        Exchange(
            "zyz"[i], backs[i], back_mids[i], homes[i],
            send1.at[4 + i], recv1.at[4 + i], send2.at[4 + i], recv2.at[4 + i],
        )
        for i in range(3)
    ]
    for stream in outward:
        stream.phase1()
    for stream in outward:
        stream.phase2()

    row, col = iota((CH, CH), 0), iota((CH, CH), 1)
    same = row // BLOCK == col // BLOCK
    ra, ca = row % BLOCK, col % BLOCK
    unpack = jnp.concatenate(
        [
            jnp.where(same & (ra < 6) & (ca == 6 + ra // 3) & (ra % 3 == j), 1.0, 0.0)
            for j in range(3)
        ],
        axis=1,
    ).astype(BF16)
    repack = [
        jnp.where(same & (ra >= 6) & (ca == 3 * (ra - 6) + j), 1.0, 0.0).astype(BF16)
        for j in range(3)
    ]
    real = (iota((CH, 1), 0) % BLOCK) < SLOTS
    spot = iota((CH, 128), 1) == iota((CH, 128), 0) % BLOCK
    wg, wu, wd = weights

    def rows_of(g):
        return pl.ds(pl.multiple_of(g * CH, CH), CH)

    def unpack_group(halves, ref, g):
        rows = rows_of(g)
        chunks = []
        for j in range(3):
            chunk = get_chunk(halves, pl.ds(2 * g, 2), j)
            ref[rows, j * CH : (j + 1) * CH] = chunk
            chunks.append(chunk)
        ref[rows, 3 * CH :] = dot(unpack, jnp.concatenate(chunks, axis=0)).astype(BF16)

    for one in loads:
        one.wait()
    for stream in outward[:2]:
        stream.arrived()

    def forward(g, _):
        rows = rows_of(g)
        unpack_group(gots[:2], x_s, g)
        x = x_s[rows, :]
        pre_gate = dot(x, wg[...])
        pre_up = dot(x, wu[...])
        sig = jax.nn.sigmoid(pre_gate)
        silu = jnp.where(real, pre_gate * sig, 0.0)
        h_s[rows, :] = (silu * pre_up).astype(BF16)
        silu_s[rows, :] = silu
        a_s[rows, :] = jnp.where(real, pre_up * sig * (1.0 + pre_gate * (1.0 - sig)), 0.0)
        return 0

    lax.fori_loop(0, 4, forward, 0)
    for stream in outward[2:]:
        stream.arrived()

    def backward(g, _):
        rows = rows_of(g)
        zs = pl.ds(2 * g, 2)
        unpack_group(gots[2:], s_s, g)
        hgrad = dot(s_s[rows, :], wd[...], ((1,), (1,)))
        d_gate = (hgrad * a_s[rows, :]).astype(BF16)
        d_up = (hgrad * silu_s[rows, :]).astype(BF16)
        dg_s[rows, :] = d_gate
        du_s[rows, :] = d_up
        product = jnp.sum(h_s[rows, :].astype(F32) * hgrad, axis=1, keepdims=True)
        spots = jnp.where(spot, product, 0.0).reshape(CH // BLOCK, BLOCK, 128)
        backs[2][zs] = jnp.sum(spots, axis=1).reshape(2, 8, 2, 1, 128)

        def route(cols):
            return dot(d_gate, wg[cols, :], ((1,), (1,))) + dot(d_up, wu[cols, :], ((1,), (1,)))

        tail = route(slice(3 * CH, 4 * CH)).astype(BF16)
        for j in range(3):
            part = route(slice(j * CH, (j + 1) * CH)) + dot(repack[j], tail)
            put_chunk(backs[:2], zs, j, part.astype(BF16))

        @pl.when(g > 0)
        def _():
            for stream in homeward:
                stream.group1(g - 1)

        return 0

    lax.fori_loop(0, 4, backward, 0)

    def grads(i, _):
        cols = pl.ds(pl.multiple_of(i * CH, CH), CH)
        x = x_s[:, cols]
        parts[0][i] = dot(x, dg_s[...], ((0,), (0,))).astype(BF16)
        parts[1][i] = dot(x, du_s[...], ((0,), (0,))).astype(BF16)
        parts[2][i] = dot(h_s[...], s_s[:, cols], ((0,), (0,))).astype(BF16)
        return 0

    lax.fori_loop(0, 4, grads, 0)
    for stream in homeward:
        stream.group1(3)

    def scatter_copy(k, i):
        target = (dp + i) % 4
        return pltpu.make_async_remote_copy(
            src_ref=parts[k].at[target],
            dst_ref=lands[k].at[dp],
            send_sem=send3.at[k, i],
            recv_sem=recv3.at[k],
            device_id=(target, me),
            device_id_type=pl.DeviceIdType.MESH,
        )

    for k in range(3):
        for i in (1, 3, 2):
            scatter_copy(k, i).start()
        pltpu.make_async_copy(parts[k].at[dp], lands[k].at[dp], recv3.at[k]).start()
    for stream in homeward:
        stream.phase2()
    for stream in homeward:
        stream.arrived()
    for stream in outward:
        stream.sent()
    for stream in homeward:
        stream.sent(grouped=True)
    for k in range(3):
        pltpu.make_async_copy(lands[k], lands[k], recv3.at[k]).wait()
        for i in (1, 3, 2):
            scatter_copy(k, i).wait_send()


def local(kernel, out_shape, args, scratch=(), name=None):
    return pl.pallas_call(
        kernel,
        out_shape=out_shape,
        in_specs=[VMEM] * len(args),
        out_specs=jax.tree.map(lambda _: VMEM, out_shape),
        scratch_shapes=scratch,
        compiler_params=pltpu.CompilerParams(vmem_limit_bytes=48 << 20),
        name=name,
    )(*args)


def shape(*dims, dtype=BF16):
    return jax.ShapeDtypeStruct(dims, dtype)


def shards(tokens, grad_out, expert_ids, gate_weight, w_gate, w_up, w_down):
    ids, gates = expert_ids.T, gate_weight.T
    send = local(pack_kernel, (shape(128, BLOCK, 384),) * 4, (ids, gates, tokens, grad_out), name="pack")
    half, small = (8, 8, 2, BLOCK, 384), (8, 8, 2, 1, 128)
    blocks = [(half, BF16), (half, BF16), (small, F32)]
    parts = [((4, 256, 384), BF16), ((4, 256, 384), BF16), ((4, 384, 256), BF16)]
    weights = [((1024, 384), BF16), ((1024, 384), BF16), ((384, 1024), BF16)]
    rows = [((ROWS, 1024), BF16)] * 2 + [((ROWS, 384), F32)] * 2 + [((ROWS, 384), BF16)] * 3
    sem = pltpu.SemaphoreType.DMA
    *home, land_gate, land_up, land_down = pl.pallas_call(
        main_kernel,
        out_shape=[shape(*dims, dtype=kind) for dims, kind in blocks + parts],
        in_specs=[VMEM] * 4 + [pl.BlockSpec(memory_space=pl.ANY)] * 3,
        out_specs=[VMEM] * 6,
        scratch_shapes=[
            pltpu.VMEM(dims, kind)
            for dims, kind in [(half, BF16)] * 8 + weights + rows + blocks * 2 + parts
        ]
        + [sem((7, 32)), sem((7,)), sem((7, 16)), sem((7,)), sem((3, 4)), sem((3,)), sem((3,))],
        compiler_params=pltpu.CompilerParams(
            collective_id=0, has_side_effects=True, vmem_limit_bytes=50 << 20
        ),
        name="main",
    )(*[a.reshape(half) for a in send], w_gate[0], w_up[0], w_down[0])
    home = [a.reshape(128, *a.shape[3:]) for a in home]
    sums = (land_gate, land_up, land_down)
    wide = shape(1, 256, 384, dtype=F32)
    grad_tokens, grad_gate, *grads = local(
        combine_kernel,
        (shape(128, 1024), shape(4, 128), wide, wide, shape(1, 384, 256, dtype=F32)),
        (ids, gates, *home, *sums),
        name="combine",
    )
    return (grad_tokens, grad_gate.T, *grads)


def solution(mesh):
    rows = P(("dp", "expert"), None)
    weights = P("expert", None, None)
    return jax.shard_map(
        shards,
        mesh=mesh,
        in_specs=(rows, rows, rows, rows, weights, weights, weights),
        out_specs=(rows, rows, P("expert", "dp", None), P("expert", "dp", None), P("expert", None, "dp")),
        check_vma=False,
    )
```

time: 157 us -> 149 us (0.949)
  Pallas kernels: 151 us -> 141 us
  local copies, waits for them, and re-layouts: 4.37 us -> 6.13 us
    pallas_call x3 -> x2, Pallas kernels: 19.4 us -> 4.12 us  [local(): pl.pallas_call(kernel, out_shape=out_shape, in_specs=[VMEM] * len(args),...]
    pallas_call x2 -> x1, Pallas kernels: 131 us -> 137 us  [shards(): pl.pallas_call(main_kernel, out_shape=[shape(*dims, dtype=kind) for dims,...]
    unnamed x12 -> x16, local copies, waits for them, and re-layouts: 4.37 us -> 6.13 us
where the time goes in v3:
time: 149 us; the launch traced here: 148 us
  Pallas kernels  141 us (95%)
  local copies, waits for them, and re-layouts  6.13 us (4%)
    pallas_call x1, Pallas kernels, shards(): pl.pallas_call(main_kernel, out_shape=[shape(*dims, dtype=kind) for dims,...  137 us
    unnamed x16, local copies, waits for them, and re-layouts  6.13 us
    pallas_call x2, Pallas kernels, local(): pl.pallas_call(kernel, out_shape=out_shape, in_specs=[VMEM] * len(args),...  4.12 us

profile of v3, /device:TPU:1, one launch (start us, length us, event | category | flops | bytes accessed | tf_op | source)
XLA Modules:
  0.0 147.5 jit_solution(16493442198146062840)
XLA Ops:
  0.6 0.0 copy-start.6
  0.6 0.0 copy-start.7
  0.7 0.7 copy-done.6
  1.3 0.0 copy-done.7
  1.3 0.0 copy-start.4
  1.3 0.9 copy-done.4
  2.3 0.0 copy-start.5
  2.3 0.9 copy-done.5
  3.2 1.5 pack.1
  4.7 0.0 copy-start
  4.7 0.9 copy-done
  5.6 0.0 copy-start.1
  5.6 0.9 copy-done.1
  6.5 0.0 copy-start.2
  6.5 0.9 copy-done.2
  7.4 0.0 copy-start.3
  7.4 0.9 copy-done.3
  8.2 136.6 %main.1 = (bf16[8,8,2,8,384]{4,3,2,1,0:T(8,128)(2,1)S(1)}, bf16[8,8,2,8,384]{4,3,2,1,0:T(8,128)(2,1)S(1)}, f32[8,8,2,1,128]{4,3,2,1,0:T(1,128)S(1)}, bf16[4,256,...) custom-call(bf16[8,8,2,8,384]{4,3,2,1,0:T(8,128)(2,1)} %bitcast.15, ...), custom_call_target="tpu_custom_call" | custom-call | tf_op jit(solution)/shard_map/main/pallas_call | solution.py:453
  144.8 2.7 %combine.1 = (bf16[128,1024]{1,0:T(8,128)(2,1)}, bf16[4,128]{1,0:T(4,128)(2,1)}, f32[1,256,384]{2,1,0:T(8,128)}, f32[1,256,384]{2,1,0:T(8,128)}, f32[1,384,256]{2,1,0:T(8,128)}) custom-call(s32[4,128]{1,0:T(4,128)S(1)} %bitcast.21, bf16[4,128]{1,0:T(4,128)(2,1)S(1)} %bitcast.23, bf16[128,8,384]{2,1,0:T(8,128)(2,1)S(1)} %bitcast.13, ...), custom_call_target="tpu_custom_call" | custom-call | tf_op jit(solution)/shard_map/combine/pallas_call | solution.py:429
Async XLA Ops:
  0.6 0.7 copy-start.6
  0.6 0.7 copy-start.7
  1.3 0.9 copy-start.4
  2.3 0.9 copy-start.5
  4.7 0.9 copy-start
  5.6 0.9 copy-start.1
  6.5 0.9 copy-start.2
  7.4 0.9 copy-start.3

commit v4 on v3

--- a/solution.py
+++ b/solution.py
@@ -70,29 +70,6 @@
     if j == 1:
         return jnp.concatenate([get(low, 256, 384), get(high, 0, 128)], axis=1)
     return get(high, 128, 384)
-
-
-def pack_kernel(ids_ref, gate_ref, tok_ref, up_ref, xa_ref, xb_ref, sa_ref, sb_ref):
-    ids = ids_ref[...]
-    _, main, tails, spread = one_hots(ids)
-    gates = gate_ref[...].astype(F32)
-    experts = iota((128, 128), 0)
-    gate_of = jnp.zeros((128, 128), F32)
-    for k in range(4):
-        gate_of = gate_of + jnp.where(ids[k : k + 1, :] == experts, gates[k : k + 1, :], 0.0)
-    gate_rows = dot(spread, gate_of.astype(BF16))
-    for j in range(3):
-        gate_col = jnp.sum((main + tails[j]) * gate_rows, axis=1, keepdims=True)
-        pick = jnp.concatenate([main.astype(BF16), tails[j].astype(BF16)], axis=1)
-        for which, ref in enumerate((tok_ref, up_ref)):
-            both = jnp.concatenate(
-                [ref[:, j * CH : (j + 1) * CH], ref[:, 3 * CH : 4 * CH]], axis=0
-            )
-            rows = dot(pick, both)
-            if which == 1:
-                rows = rows * gate_col
-            halves = ((xa_ref, xb_ref), (sa_ref, sb_ref))[which]
-            put_chunk(halves, slice(None), j, rows.astype(BF16))
 
 
 def combine_kernel(
@@ -206,18 +183,9 @@
             device_id_type=pl.DeviceIdType.MESH,
         )
 
-    def phase1(self):
-        along = self.along()
-
-        def one(i, _):
-            self.copy1((along + ring_step(i)) % 8).start()
-            return 0
-
-        lax.fori_loop(1, 8, one, 0)
-        pltpu.make_async_copy(self.slab(along), self.mid.at[along], self.recv1).start()
-
-    def phase2(self):
-        pltpu.make_async_copy(self.mid, self.mid, self.recv1).wait()
+    def phase2(self, received=True):
+        if received:
+            pltpu.make_async_copy(self.mid, self.mid, self.recv1).wait()
 
         def one(i, _):
             self.copy2(i).start()
@@ -230,10 +198,10 @@
     def arrived(self):
         pltpu.make_async_copy(self.dst, self.dst, self.recv2).wait()
 
-    def sent(self, grouped=False):
+    def sent1(self):
         def one(i, _):
             p = (self.along() + i) % 8
-            if grouped and self.route == "y":
+            if self.route == "y":
                 for g in range(4):
                     self.piece1(p, g).wait_send()
             else:
@@ -242,6 +210,7 @@
 
         lax.fori_loop(1, 8, one, 0)
 
+    def sent2(self):
         def two(i, _):
             self.copy2(i).wait_send()
             return 0
@@ -267,40 +236,169 @@
     signal((dp, z * 16 + y * 2 + 1 - c))
     for i in range(1, 4):
         signal(((dp + i) % 4, me))
-    pl.semaphore_wait(barrier, 32)
+    return barrier
+
+
+class Ring:
+    def __init__(self, number, inputs, ids, gates, held, held_ids, held_gates, xs, ss, send, recv, few, meta):
+        self.number, self.inputs, self.ids, self.gates = number, inputs, ids, gates
+        self.held, self.held_ids, self.held_gates = held, held_ids, held_gates
+        self.xs, self.ss, self.send, self.recv, self.few, self.meta = xs, ss, send, recv, few, meta
+        self.dp, me = lax.axis_index("dp"), lax.axis_index("expert")
+        self.z, self.y, self.c = me // 16, (me // 2) % 8, me % 2
+        self.at = self.y if number else self.z
+
+    def device(self, p):
+        if self.number:
+            return (self.dp, self.z * 16 + p * 2 + self.c)
+        return (self.dp, p * 16 + self.y * 2 + self.c)
+
+    def own(self, part):
+        return self.inputs[part].at[:, pl.ds(512 * self.number, 512)]
+
+    def copy(self, part, way, step):
+        block = (self.at - way * (step - 1) + 8) % 8
+        which = part * 2 + (way > 0)
+        return pltpu.make_async_remote_copy(
+            src_ref=self.own(part) if step == 1 else self.held.at[block, part],
+            dst_ref=self.held.at[block, part],
+            send_sem=self.send.at[which, step],
+            recv_sem=self.recv.at[which, step],
+            device_id=self.device((self.at + way + 8) % 8),
+            device_id_type=pl.DeviceIdType.MESH,
+        )
+
+    def arrived(self, part, way, step):
+        block = self.held.at[(self.at - way * step + 8) % 8, part]
+        pltpu.make_async_copy(block, block, self.recv.at[part * 2 + (way > 0), step]).wait()
+
+    def small(self, i):
+        for k, (src, dst) in enumerate(((self.ids, self.held_ids), (self.gates, self.held_gates))):
+            yield pltpu.make_async_remote_copy(
+                src_ref=src,
+                dst_ref=dst.at[self.at],
+                send_sem=self.few.at[k, i],
+                recv_sem=self.meta.at[k],
+                device_id=self.device((self.at + i) % 8),
+                device_id_type=pl.DeviceIdType.MESH,
+            )
+
+    def pick(self, block, ids, gates):
+        row = iota((128, 128), 0)
+        place, receiver = (row % BLOCK).astype(F32), row // BLOCK
+        if self.number:
+            expert = receiver // 2 * 16 + self.y * 2 + receiver % 2
+        else:
+            expert = self.z * 16 + receiver
+        named, gate = jnp.zeros((128, 128), F32), jnp.zeros((128, 128), F32)
+        for k in range(4):
+            hit = ids[k : k + 1, :] == expert
+            named = jnp.where(hit, 1.0, named)
+            gate = jnp.where(hit, gates[k : k + 1, :], gate)
+        earlier = jnp.where(row < iota((128, 128), 1), 1.0, 0.0).astype(BF16)
+        rank = jnp.where(named > 0.5, dot(named.astype(BF16), earlier), -1.0)
+        main = jnp.where((rank == place) & (place < 5.5), 1.0, 0.0)
+        held = self.held
+
+        def chunk(j):
+            return jnp.concatenate(
+                [held[block, part, :, j * 128 : (j + 1) * 128] for part in range(2)], axis=1
+            )
+
+        last = chunk(3)
+        for j in range(3):
+            tail = jnp.where((rank == 3.0 * (place - 6.0) + j) & (place > 5.5), 1.0, 0.0)
+            scale = jnp.sum((main + tail) * gate, axis=1, keepdims=True)
+            choice = jnp.concatenate([main.astype(BF16), tail.astype(BF16)], axis=1)
+            rows = dot(choice, jnp.concatenate([chunk(j), last], axis=0))
+            lanes = slice(j * 128, (j + 1) * 128)
+            self.xs[block, :, :, :, lanes] = rows[:, :128].astype(BF16).reshape(8, 2, 8, 128)
+            self.ss[block, :, :, :, lanes] = (
+                (rows[:, 128:] * scale).astype(BF16).reshape(8, 2, 8, 128)
+            )
+
+    def pick_step(self, way, step):
+        block = (self.at - way * step + 8) % 8
+        self.pick(block, self.held_ids[block], self.held_gates[block].astype(F32))
 
 
 def main_kernel(*refs):
     refs = list(refs)
     take = lambda count: [refs.pop(0) for _ in range(count)]
-    sends, weights_hbm = take(4), take(3)
+    (ids, gates), inputs, weights_hbm = take(2), take(2), take(3)
     homes, lands = take(3), take(3)
+    helds, held_ids, held_gates, (my_ids, my_gates) = take(2), take(2), take(2), take(2)
     mids, gots, weights = take(4), take(4), take(3)
     x_s, s_s, a_s, silu_s, dg_s, du_s, h_s = take(7)
     backs, back_mids, parts = take(3), take(3), take(3)
     send1, recv1, send2, recv2, send3, recv3, load = take(7)
+    ring_send, ring_recv, few, meta, mine = take(5)
+    barrier = greet()
     dp, me = lax.axis_index("dp"), lax.axis_index("expert")
-    loads = [pltpu.make_async_copy(weights_hbm[i], weights[i], load.at[i]) for i in range(3)]
-    for one in loads:
-        one.start()
-    greet()
+    rings = [
+        Ring(
+            t, inputs, ids, gates, helds[t], held_ids[t], held_gates[t], mids[t], mids[2 + t],
+            ring_send.at[t], ring_recv.at[t], few.at[t], meta.at[t],
+        )
+        for t in range(2)
+    ]
     outward = [
-        Exchange(
-            "zyzy"[i], sends[i], mids[i], gots[i], send1.at[i], recv1.at[i], send2.at[i], recv2.at[i]
-        )
+        Exchange("zyzy"[i], None, mids[i], gots[i], None, None, send2.at[i], recv2.at[i])
         for i in range(4)
     ]
     homeward = [
         Exchange(
             "zyz"[i], backs[i], back_mids[i], homes[i],
-            send1.at[4 + i], recv1.at[4 + i], send2.at[4 + i], recv2.at[4 + i],
+            send1.at[i], recv1.at[i], send2.at[4 + i], recv2.at[4 + i],
         )
         for i in range(3)
     ]
+    locals_ = [
+        pltpu.make_async_copy(ids, my_ids, mine.at[0]),
+        pltpu.make_async_copy(gates, my_gates, mine.at[1]),
+    ] + [
+        pltpu.make_async_copy(ring.own(part), ring.held.at[ring.at, part], mine.at[2 + 2 * t + part])
+        for t, ring in enumerate(rings)
+        for part in range(2)
+    ]
+    loads = [pltpu.make_async_copy(weights_hbm[i], weights[i], load.at[i]) for i in range(3)]
+    for one in locals_ + loads:
+        one.start()
+    for ring in rings:
+        pltpu.make_async_copy(ids, ring.held_ids.at[ring.at], ring.meta.at[0]).start()
+        pltpu.make_async_copy(gates, ring.held_gates.at[ring.at], ring.meta.at[1]).start()
+    for one in locals_:
+        one.wait()
+    for ring in rings:
+        ring.pick(ring.at, my_ids[...], my_gates[...].astype(F32))
+    pl.semaphore_wait(barrier, 32)
+    for i in range(1, 8):
+        for ring in rings:
+            for one in ring.small(i):
+                one.start()
+    for part in range(2):
+        for ring in rings:
+            for way in (1, -1):
+                ring.copy(part, way, 1).start()
+    for ring in rings:
+        pltpu.make_async_copy(ring.held_ids, ring.held_ids, ring.meta.at[0]).wait()
+        pltpu.make_async_copy(ring.held_gates, ring.held_gates, ring.meta.at[1]).wait()
+    for step in range(2, 5):
+        for part in range(2):
+            for ring in rings:
+                for way in (1, -1):
+                    ring.arrived(part, way, step - 1)
+                    if step < 4 or (way > 0) == (part == 0):
+                        ring.copy(part, way, step).start()
+        for ring in rings:
+            for way in (1, -1):
+                ring.pick_step(way, step - 1)
+    for ring in rings:
+        ring.arrived(0, 1, 4)
+        ring.arrived(1, -1, 4)
+        ring.pick_step(1, 4)
     for stream in outward:
-        stream.phase1()
-    for stream in outward:
-        stream.phase2()
+        stream.phase2(received=False)
 
     row, col = iota((CH, CH), 0), iota((CH, CH), 1)
     same = row // BLOCK == col // BLOCK
@@ -324,13 +422,17 @@
         return pl.ds(pl.multiple_of(g * CH, CH), CH)
 
     def unpack_group(halves, ref, g):
-        rows = rows_of(g)
+        rows, zs = rows_of(g), pl.ds(2 * g, 2)
         chunks = []
         for j in range(3):
-            chunk = get_chunk(halves, pl.ds(2 * g, 2), j)
-            ref[rows, j * CH : (j + 1) * CH] = chunk
-            chunks.append(chunk)
-        ref[rows, 3 * CH :] = dot(unpack, jnp.concatenate(chunks, axis=0)).astype(BF16)
+            lanes = slice(j * 128, (j + 1) * 128)
+            low, high = (half[zs, :, :, :, lanes].reshape(CH, 128) for half in halves)
+            ref[rows, lanes] = low
+            ref[rows, 512 + j * 128 : 512 + (j + 1) * 128] = high
+            chunks.append(jnp.concatenate([low, high], axis=1))
+        last = dot(unpack, jnp.concatenate(chunks, axis=0)).astype(BF16)
+        ref[rows, 384:512] = last[:, :128]
+        ref[rows, 896:1024] = last[:, 128:]
 
     for one in loads:
         one.wait()
@@ -415,10 +517,20 @@
         stream.phase2()
     for stream in homeward:
         stream.arrived()
+    for ring in rings:
+        for i in range(1, 8):
+            for one in ring.small(i):
+                one.wait_send()
+        for step in range(1, 5):
+            for part in range(2):
+                for way in (1, -1):
+                    if step < 4 or (way > 0) == (part == 0):
+                        ring.copy(part, way, step).wait_send()
     for stream in outward:
-        stream.sent()
+        stream.sent2()
     for stream in homeward:
-        stream.sent(grouped=True)
+        stream.sent1()
+        stream.sent2()
     for k in range(3):
         pltpu.make_async_copy(lands[k], lands[k], recv3.at[k]).wait()
         for i in (1, 3, 2):
@@ -443,28 +555,30 @@
 
 def shards(tokens, grad_out, expert_ids, gate_weight, w_gate, w_up, w_down):
     ids, gates = expert_ids.T, gate_weight.T
-    send = local(pack_kernel, (shape(128, BLOCK, 384),) * 4, (ids, gates, tokens, grad_out), name="pack")
     half, small = (8, 8, 2, BLOCK, 384), (8, 8, 2, 1, 128)
     blocks = [(half, BF16), (half, BF16), (small, F32)]
     parts = [((4, 256, 384), BF16), ((4, 256, 384), BF16), ((4, 384, 256), BF16)]
     weights = [((1024, 384), BF16), ((1024, 384), BF16), ((384, 1024), BF16)]
     rows = [((ROWS, 1024), BF16)] * 2 + [((ROWS, 384), F32)] * 2 + [((ROWS, 384), BF16)] * 3
+    ring = [((8, 2, 128, 512), BF16)] * 2 + [((8, 4, 128), jnp.int32)] * 2
+    ring += [((8, 4, 128), BF16)] * 2 + [((4, 128), jnp.int32), ((4, 128), BF16)]
     sem = pltpu.SemaphoreType.DMA
     *home, land_gate, land_up, land_down = pl.pallas_call(
         main_kernel,
         out_shape=[shape(*dims, dtype=kind) for dims, kind in blocks + parts],
-        in_specs=[VMEM] * 4 + [pl.BlockSpec(memory_space=pl.ANY)] * 3,
+        in_specs=[pl.BlockSpec(memory_space=pl.ANY)] * 7,
         out_specs=[VMEM] * 6,
         scratch_shapes=[
             pltpu.VMEM(dims, kind)
-            for dims, kind in [(half, BF16)] * 8 + weights + rows + blocks * 2 + parts
+            for dims, kind in ring + [(half, BF16)] * 8 + weights + rows + blocks * 2 + parts
         ]
-        + [sem((7, 32)), sem((7,)), sem((7, 16)), sem((7,)), sem((3, 4)), sem((3,)), sem((3,))],
+        + [sem((3, 32)), sem((3,)), sem((7, 16)), sem((7,)), sem((3, 4)), sem((3,)), sem((3,))]
+        + [sem((2, 4, 5)), sem((2, 4, 5)), sem((2, 2, 8)), sem((2, 2)), sem((6,))],
         compiler_params=pltpu.CompilerParams(
             collective_id=0, has_side_effects=True, vmem_limit_bytes=50 << 20
         ),
         name="main",
-    )(*[a.reshape(half) for a in send], w_gate[0], w_up[0], w_down[0])
+    )(ids, gates, tokens, grad_out, w_gate[0], w_up[0], w_down[0])
     home = [a.reshape(128, *a.shape[3:]) for a in home]
     sums = (land_gate, land_up, land_down)
     wide = shape(1, 256, 384, dtype=F32)

time: 149 us -> 135 us (0.906)
  Pallas kernels: 141 us -> 130 us
  local copies, waits for them, and re-layouts: 6.13 us -> 3.7 us
    pallas_call x1, Pallas kernels: 137 us -> 127 us  [shards(): pl.pallas_call(main_kernel, out_shape=[shape(*dims, dtype=kind) for dims,...]
    unnamed x16 -> x10, local copies, waits for them, and re-layouts: 6.13 us -> 3.7 us
    pallas_call x2 -> x1, Pallas kernels: 4.12 us -> 2.77 us  [local(): pl.pallas_call(kernel, out_shape=out_shape, in_specs=[VMEM] * len(args),...]
where the time goes in v4:
time: 135 us; the launch traced here: 134 us
  Pallas kernels  130 us (96%)
  local copies, waits for them, and re-layouts  3.7 us (3%)
    pallas_call x1, Pallas kernels, shards(): pl.pallas_call(main_kernel, out_shape=[shape(*dims, dtype=kind) for dims,...  127 us
    unnamed x10, local copies, waits for them, and re-layouts  3.7 us
    pallas_call x1, Pallas kernels, local(): pl.pallas_call(kernel, out_shape=out_shape, in_specs=[VMEM] * len(args),...  2.77 us

profile of v4, /device:TPU:1, one launch (start us, length us, event | category | flops | bytes accessed | tf_op | source)
XLA Modules:
  0.0 134.3 jit_solution(11972567723694715715)
XLA Ops:
  0.6 0.0 copy-start.3
  0.6 0.0 copy-start.4
  0.7 0.7 copy-done.3
  1.3 0.0 copy-done.4
  1.3 0.0 copy-start.1
  1.3 0.9 copy-done.1
  2.3 0.0 copy-start.2
  2.3 0.9 copy-done.2
  3.2 127.2 %main.1 = (bf16[8,8,2,8,384]{4,3,2,1,0:T(8,128)(2,1)S(1)}, bf16[8,8,2,8,384]{4,3,2,1,0:T(8,128)(2,1)S(1)}, f32[8,8,2,1,128]{4,3,2,1,0:T(1,128)S(1)}, bf16[4,256,...) custom-call(s32[4,128]{1,0:T(4,128)S(1)} %bitcast.12, ...), custom_call_target="tpu_custom_call" | custom-call | tf_op jit(solution)/shard_map/main/pallas_call | solution.py:566
  130.4 0.0 copy-start
  130.5 1.1 copy-done
  131.6 2.8 %combine.1 = (bf16[128,1024]{1,0:T(8,128)(2,1)}, bf16[4,128]{1,0:T(4,128)(2,1)}, f32[1,256,384]{2,1,0:T(8,128)}, f32[1,256,384]{2,1,0:T(8,128)}, f32[1,384,256]{2,1,0:T(8,128)}) custom-call(s32[4,128]{1,0:T(4,128)S(1)} %bitcast.13, bf16[4,128]{1,0:T(4,128)(2,1)S(1)} %bitcast.15, bf16[128,8,384]{2,1,0:T(8,128)(2,1)S(1)} %bitcast.9, ...), custom_call_target="tpu_custom_call" | custom-call | tf_op jit(solution)/shard_map/combine/pallas_call | solution.py:541
Async XLA Ops:
  0.6 0.7 copy-start.3
  0.6 0.7 copy-start.4
  1.3 0.9 copy-start.1
  2.3 0.9 copy-start.2
  130.4 1.1 copy-start

commit v5 on v4

--- a/solution.py
+++ b/solution.py
@@ -12,6 +12,7 @@
 BLOCK = 8
 ROWS = 1024
 CH = 256
+SPLIT = 1
 VMEM = pl.BlockSpec(memory_space=pltpu.VMEM)
 
 
@@ -42,48 +43,40 @@
     return rank, main, tails, spread
 
 
-def put_chunk(halves, blocks, j, rows):
-    low, high = halves
-    lead = low.at[blocks].shape[:-1]
-
-    def put(ref, at, value):
-        ref[(blocks, *[slice(None)] * (len(lead) - 1), at)] = value.reshape(*lead, value.shape[1])
-
-    if j == 0:
-        put(low, slice(0, 256), rows)
-    elif j == 1:
-        put(low, slice(256, 384), rows[:, 0:128])
-        put(high, slice(0, 128), rows[:, 128:256])
-    else:
-        put(high, slice(128, 384), rows)
-
-
-def get_chunk(halves, blocks, j):
-    low, high = halves
-
-    def get(ref, lo, hi):
-        at = (blocks, *[slice(None)] * (len(ref.shape) - 2), slice(lo, hi))
-        return ref[at].reshape(-1, hi - lo)
-
-    if j == 0:
-        return get(low, 0, 256)
+def put_chunk(pieces, pair, j, rows):
+    first, third, low, high = pieces
+    for i, at in enumerate(pair):
+        half = rows[i * 128 : (i + 1) * 128]
+        if j == 1:
+            low[at] = half[:, :128].reshape(8, 2, BLOCK, 128)
+            high[at] = half[:, 128:].reshape(8, 2, BLOCK, 128)
+        else:
+            (third if j else first)[at] = half.reshape(8, 2, BLOCK, CH)
+
+
+def get_chunk(pieces, j):
+    first, third, low, high = pieces
     if j == 1:
-        return jnp.concatenate([get(low, 256, 384), get(high, 0, 128)], axis=1)
-    return get(high, 128, 384)
+        return jnp.concatenate(
+            [low[...].reshape(ROWS, 128), high[...].reshape(ROWS, 128)], axis=1
+        )
+    return (third if j else first)[...].reshape(ROWS, CH)
 
 
 def combine_kernel(
-    ids_ref, gate_ref, ba_ref, bb_ref, p_ref, rg_ref, ru_ref, rd_ref,
-    tok_ref, gate_out_ref, gg_ref, gu_ref, gd_ref
+    ids_ref, gate_ref, *refs
 ):
-    for part, total in ((rg_ref, gg_ref), (ru_ref, gu_ref), (rd_ref, gd_ref)):
-        total[0] = sum(part[i].astype(F32) for i in range(1, 4)) + part[0].astype(F32)
+    pieces, p_ref, sums = refs[:4], refs[4], refs[5:8]
+    tok_ref, gate_out_ref, *grads = refs[8:13]
+    copies = [pltpu.make_async_copy(sums[i], grads[i], refs[13].at[i]) for i in range(3)]
+    for copy in copies:
+        copy.start()
     ids = ids_ref[...]
     rank, main, tails, _ = one_hots(ids)
     main = main.astype(BF16)
     last = jnp.zeros((128, CH), F32)
     for j in range(3):
-        part = get_chunk((ba_ref, bb_ref), slice(None), j)
+        part = get_chunk(pieces, j)
         tok_ref[:, j * CH : (j + 1) * CH] = dot(main, part, ((0,), (0,))).astype(BF16)
         last = last + dot(tails[j].astype(BF16), part, ((0,), (0,)))
     tok_ref[:, 3 * CH :] = last.astype(BF16)
@@ -95,6 +88,8 @@
     for k in range(4):
         total = jnp.sum(jnp.where(ids[k : k + 1, :] == experts, mine, 0.0), axis=0, keepdims=True)
         gate_out_ref[k : k + 1, :] = (total / gates[k : k + 1, :]).astype(BF16)
+    for copy in copies:
+        copy.wait()
 
 
 def ring_step(i):
@@ -134,40 +129,38 @@
             device_id_type=pl.DeviceIdType.MESH,
         )
 
-    def piece1(self, p, g):
-        zs = pl.ds(2 * g, 2)
+    def piece1(self, p, at):
         return pltpu.make_async_remote_copy(
-            src_ref=self.src.at[zs, p],
-            dst_ref=self.mid.at[self.y, zs],
-            send_sem=self.send1.at[8 * g + p],
+            src_ref=self.src.at[at, p],
+            dst_ref=self.mid.at[self.y, at],
+            send_sem=self.send1.at[8 * at + p],
             recv_sem=self.recv1,
             device_id=(self.dp, self.first(p)),
             device_id_type=pl.DeviceIdType.MESH,
         )
 
-    def group1(self, g):
-        if self.route == "z":
-            for p in (2 * g, 2 * g + 1):
-
-                @pl.when(p != self.z)
+    def group1(self, pair):
+        for at in pair:
+            if self.route == "z":
+
+                @pl.when(at != self.z)
                 def _():
-                    self.copy1(p).start()
-
-                @pl.when(p == self.z)
+                    self.copy1(at).start()
+
+                @pl.when(at == self.z)
                 def _():
-                    pltpu.make_async_copy(self.slab(p), self.mid.at[p], self.recv1).start()
-
-        else:
-
-            def one(i, _):
-                self.piece1((self.y + ring_step(i)) % 8, g).start()
-                return 0
-
-            lax.fori_loop(1, 8, one, 0)
-            zs = pl.ds(2 * g, 2)
-            pltpu.make_async_copy(
-                self.src.at[zs, self.y], self.mid.at[self.y, zs], self.recv1
-            ).start()
+                    pltpu.make_async_copy(self.slab(at), self.mid.at[at], self.recv1).start()
+
+            else:
+
+                def one(i, _):
+                    self.piece1((self.y + ring_step(i)) % 8, at).start()
+                    return 0
+
+                lax.fori_loop(1, 8, one, 0)
+                pltpu.make_async_copy(
+                    self.src.at[at, self.y], self.mid.at[self.y, at], self.recv1
+                ).start()
 
     def copy2(self, i):
         across = self.y if self.route == "z" else self.z
@@ -183,6 +176,16 @@
             device_id_type=pl.DeviceIdType.MESH,
         )
 
+    def phase1(self):
+        along = self.along()
+
+        def one(i, _):
+            self.copy1((along + ring_step(i)) % 8).start()
+            return 0
+
+        lax.fori_loop(1, 8, one, 0)
+        pltpu.make_async_copy(self.slab(along), self.mid.at[along], self.recv1).start()
+
     def phase2(self, received=True):
         if received:
             pltpu.make_async_copy(self.mid, self.mid, self.recv1).wait()
@@ -198,12 +201,12 @@
     def arrived(self):
         pltpu.make_async_copy(self.dst, self.dst, self.recv2).wait()
 
-    def sent1(self):
+    def sent1(self, grouped):
         def one(i, _):
             p = (self.along() + i) % 8
-            if self.route == "y":
-                for g in range(4):
-                    self.piece1(p, g).wait_send()
+            if grouped and self.route == "y":
+                for at in range(8):
+                    self.piece1(p, at).wait_send()
             else:
                 self.copy1(p).wait_send()
             return 0
@@ -256,21 +259,30 @@
     def own(self, part):
         return self.inputs[part].at[:, pl.ds(512 * self.number, 512)]
 
-    def copy(self, part, way, step):
+    def piece(self, block, q):
+        count = 128 // SPLIT
+        return self.held.at[block, q // SPLIT, pl.ds(q % SPLIT * count, count)]
+
+    def own_piece(self, q):
+        count = 128 // SPLIT
+        rows = pl.ds(q % SPLIT * count, count)
+        return self.inputs[q // SPLIT].at[rows, pl.ds(512 * self.number, 512)]
+
+    def copy(self, q, way, step):
         block = (self.at - way * (step - 1) + 8) % 8
-        which = part * 2 + (way > 0)
+        which = q * 2 + (way > 0)
         return pltpu.make_async_remote_copy(
-            src_ref=self.own(part) if step == 1 else self.held.at[block, part],
-            dst_ref=self.held.at[block, part],
+            src_ref=self.own_piece(q) if step == 1 else self.piece(block, q),
+            dst_ref=self.piece(block, q),
             send_sem=self.send.at[which, step],
             recv_sem=self.recv.at[which, step],
             device_id=self.device((self.at + way + 8) % 8),
             device_id_type=pl.DeviceIdType.MESH,
         )
 
-    def arrived(self, part, way, step):
-        block = self.held.at[(self.at - way * step + 8) % 8, part]
-        pltpu.make_async_copy(block, block, self.recv.at[part * 2 + (way > 0), step]).wait()
+    def arrived(self, q, way, step):
+        piece = self.piece((self.at - way * step + 8) % 8, q)
+        pltpu.make_async_copy(piece, piece, self.recv.at[q * 2 + (way > 0), step]).wait()
 
     def small(self, i):
         for k, (src, dst) in enumerate(((self.ids, self.held_ids), (self.gates, self.held_gates))):
@@ -326,11 +338,11 @@
     refs = list(refs)
     take = lambda count: [refs.pop(0) for _ in range(count)]
     (ids, gates), inputs, weights_hbm = take(2), take(2), take(3)
-    homes, lands = take(3), take(3)
-    helds, held_ids, held_gates, (my_ids, my_gates) = take(2), take(2), take(2), take(2)
+    homes, sums, (my_ids, my_gates) = take(5), take(3), take(2)
+    helds, held_ids, held_gates = take(2), take(2), take(2)
     mids, gots, weights = take(4), take(4), take(3)
     x_s, s_s, a_s, silu_s, dg_s, du_s, h_s = take(7)
-    backs, back_mids, parts = take(3), take(3), take(3)
+    backs, back_mids, parts, lands = take(5), take(5), take(3), take(3)
     send1, recv1, send2, recv2, send3, recv3, load = take(7)
     ring_send, ring_recv, few, meta, mine = take(5)
     barrier = greet()
@@ -348,10 +360,10 @@
     ]
     homeward = [
         Exchange(
-            "zyz"[i], backs[i], back_mids[i], homes[i],
+            "zyzyz"[i], backs[i], back_mids[i], homes[i],
             send1.at[i], recv1.at[i], send2.at[4 + i], recv2.at[4 + i],
         )
-        for i in range(3)
+        for i in range(5)
     ]
     locals_ = [
         pltpu.make_async_copy(ids, my_ids, mine.at[0]),
@@ -367,35 +379,36 @@
     for ring in rings:
         pltpu.make_async_copy(ids, ring.held_ids.at[ring.at], ring.meta.at[0]).start()
         pltpu.make_async_copy(gates, ring.held_gates.at[ring.at], ring.meta.at[1]).start()
+    pl.semaphore_wait(barrier, 32)
+    pieces = range(2 * SPLIT)
+    for q in pieces:
+        for ring in rings:
+            for way in (1, -1):
+                ring.copy(q, way, 1).start()
+    for i in range(1, 8):
+        for ring in rings:
+            for one in ring.small(i):
+                one.start()
     for one in locals_:
         one.wait()
     for ring in rings:
         ring.pick(ring.at, my_ids[...], my_gates[...].astype(F32))
-    pl.semaphore_wait(barrier, 32)
-    for i in range(1, 8):
-        for ring in rings:
-            for one in ring.small(i):
-                one.start()
-    for part in range(2):
-        for ring in rings:
-            for way in (1, -1):
-                ring.copy(part, way, 1).start()
-    for ring in rings:
-        pltpu.make_async_copy(ring.held_ids, ring.held_ids, ring.meta.at[0]).wait()
-        pltpu.make_async_copy(ring.held_gates, ring.held_gates, ring.meta.at[1]).wait()
     for step in range(2, 5):
-        for part in range(2):
+        for q in pieces:
             for ring in rings:
                 for way in (1, -1):
-                    ring.arrived(part, way, step - 1)
-                    if step < 4 or (way > 0) == (part == 0):
-                        ring.copy(part, way, step).start()
+                    ring.arrived(q, way, step - 1)
+                    if step < 4 or (way > 0) == (q < SPLIT):
+                        ring.copy(q, way, step).start()
         for ring in rings:
+            if step == 2:
+                pltpu.make_async_copy(ring.held_ids, ring.held_ids, ring.meta.at[0]).wait()
+                pltpu.make_async_copy(ring.held_gates, ring.held_gates, ring.meta.at[1]).wait()
             for way in (1, -1):
                 ring.pick_step(way, step - 1)
     for ring in rings:
-        ring.arrived(0, 1, 4)
-        ring.arrived(1, -1, 4)
+        for q in pieces:
+            ring.arrived(q, 1 if q < SPLIT else -1, 4)
         ring.pick_step(1, 4)
     for stream in outward:
         stream.phase2(received=False)
@@ -421,12 +434,21 @@
     def rows_of(g):
         return pl.ds(pl.multiple_of(g * CH, CH), CH)
 
+    z = me // 16
+
+    def pair_of(g):
+        far = jnp.where(g < 3, 3 - g, 4)
+        return (z + far) % 8, (z + jnp.where(g < 3, 8 - far, 0)) % 8
+
     def unpack_group(halves, ref, g):
-        rows, zs = rows_of(g), pl.ds(2 * g, 2)
+        rows, pair = rows_of(g), pair_of(g)
         chunks = []
         for j in range(3):
             lanes = slice(j * 128, (j + 1) * 128)
-            low, high = (half[zs, :, :, :, lanes].reshape(CH, 128) for half in halves)
+            low, high = (
+                jnp.concatenate([half[at, :, :, :, lanes].reshape(128, 128) for at in pair], axis=0)
+                for half in halves
+            )
             ref[rows, lanes] = low
             ref[rows, 512 + j * 128 : 512 + (j + 1) * 128] = high
             chunks.append(jnp.concatenate([low, high], axis=1))
@@ -457,8 +479,7 @@
         stream.arrived()
 
     def backward(g, _):
-        rows = rows_of(g)
-        zs = pl.ds(2 * g, 2)
+        rows, pair = rows_of(g), pair_of(g)
         unpack_group(gots[2:], s_s, g)
         hgrad = dot(s_s[rows, :], wd[...], ((1,), (1,)))
         d_gate = (hgrad * a_s[rows, :]).astype(BF16)
@@ -467,7 +488,9 @@
         du_s[rows, :] = d_up
         product = jnp.sum(h_s[rows, :].astype(F32) * hgrad, axis=1, keepdims=True)
         spots = jnp.where(spot, product, 0.0).reshape(CH // BLOCK, BLOCK, 128)
-        backs[2][zs] = jnp.sum(spots, axis=1).reshape(2, 8, 2, 1, 128)
+        spots = jnp.sum(spots, axis=1)
+        for i, at in enumerate(pair):
+            backs[4][at] = spots[i * 16 : (i + 1) * 16].reshape(8, 2, 1, 128)
 
         def route(cols):
             return dot(d_gate, wg[cols, :], ((1,), (1,))) + dot(d_up, wu[cols, :], ((1,), (1,)))
@@ -475,12 +498,12 @@
         tail = route(slice(3 * CH, 4 * CH)).astype(BF16)
         for j in range(3):
             part = route(slice(j * CH, (j + 1) * CH)) + dot(repack[j], tail)
-            put_chunk(backs[:2], zs, j, part.astype(BF16))
+            put_chunk(backs[:4], pair, j, part.astype(BF16))
 
         @pl.when(g > 0)
         def _():
-            for stream in homeward:
-                stream.group1(g - 1)
+            for stream in homeward[:2]:
+                stream.group1(pair_of(g - 1))
 
         return 0
 
@@ -495,8 +518,10 @@
         return 0
 
     lax.fori_loop(0, 4, grads, 0)
-    for stream in homeward:
-        stream.group1(3)
+    for stream in homeward[:2]:
+        stream.group1(pair_of(3))
+    for stream in homeward[2:]:
+        stream.phase1()
 
     def scatter_copy(k, i):
         target = (dp + i) % 4
@@ -515,6 +540,9 @@
         pltpu.make_async_copy(parts[k].at[dp], lands[k].at[dp], recv3.at[k]).start()
     for stream in homeward:
         stream.phase2()
+    for k in range(3):
+        pltpu.make_async_copy(lands[k], lands[k], recv3.at[k]).wait()
+        sums[k][0] = sum(lands[k][i].astype(F32) for i in range(1, 4)) + lands[k][0].astype(F32)
     for stream in homeward:
         stream.arrived()
     for ring in rings:
@@ -522,72 +550,67 @@
             for one in ring.small(i):
                 one.wait_send()
         for step in range(1, 5):
-            for part in range(2):
+            for q in pieces:
                 for way in (1, -1):
-                    if step < 4 or (way > 0) == (part == 0):
-                        ring.copy(part, way, step).wait_send()
+                    if step < 4 or (way > 0) == (q < SPLIT):
+                        ring.copy(q, way, step).wait_send()
     for stream in outward:
         stream.sent2()
-    for stream in homeward:
-        stream.sent1()
+    for i, stream in enumerate(homeward):
+        stream.sent1(grouped=i < 2)
         stream.sent2()
     for k in range(3):
-        pltpu.make_async_copy(lands[k], lands[k], recv3.at[k]).wait()
         for i in (1, 3, 2):
             scatter_copy(k, i).wait_send()
 
 
-def local(kernel, out_shape, args, scratch=(), name=None):
-    return pl.pallas_call(
-        kernel,
-        out_shape=out_shape,
-        in_specs=[VMEM] * len(args),
-        out_specs=jax.tree.map(lambda _: VMEM, out_shape),
-        scratch_shapes=scratch,
-        compiler_params=pltpu.CompilerParams(vmem_limit_bytes=48 << 20),
-        name=name,
-    )(*args)
-
-
 def shape(*dims, dtype=BF16):
     return jax.ShapeDtypeStruct(dims, dtype)
 
 
 def shards(tokens, grad_out, expert_ids, gate_weight, w_gate, w_up, w_down):
     ids, gates = expert_ids.T, gate_weight.T
+    inputs = (ids, gates, tokens, grad_out, w_gate[0], w_up[0], w_down[0])
     half, small = (8, 8, 2, BLOCK, 384), (8, 8, 2, 1, 128)
-    blocks = [(half, BF16), (half, BF16), (small, F32)]
+    lanes = [(8, 8, 2, BLOCK, n) for n in (256, 256, 128, 128)]
+    blocks = [(dims, BF16) for dims in lanes] + [(small, F32)]
     parts = [((4, 256, 384), BF16), ((4, 256, 384), BF16), ((4, 384, 256), BF16)]
+    totals = [((1, 256, 384), F32), ((1, 256, 384), F32), ((1, 384, 256), F32)]
     weights = [((1024, 384), BF16), ((1024, 384), BF16), ((384, 1024), BF16)]
     rows = [((ROWS, 1024), BF16)] * 2 + [((ROWS, 384), F32)] * 2 + [((ROWS, 384), BF16)] * 3
     ring = [((8, 2, 128, 512), BF16)] * 2 + [((8, 4, 128), jnp.int32)] * 2
-    ring += [((8, 4, 128), BF16)] * 2 + [((4, 128), jnp.int32), ((4, 128), BF16)]
+    ring += [((8, 4, 128), BF16)] * 2
+    routes = [((4, 128), jnp.int32), ((4, 128), BF16)]
     sem = pltpu.SemaphoreType.DMA
-    *home, land_gate, land_up, land_down = pl.pallas_call(
+    *home, sum_gate, sum_up, sum_down, my_ids, my_gates = pl.pallas_call(
         main_kernel,
-        out_shape=[shape(*dims, dtype=kind) for dims, kind in blocks + parts],
-        in_specs=[pl.BlockSpec(memory_space=pl.ANY)] * 7,
-        out_specs=[VMEM] * 6,
+        out_shape=[shape(*dims, dtype=kind) for dims, kind in blocks + totals + routes],
+        in_specs=[pl.BlockSpec(memory_space=pltpu.HBM)] * 7,
+        out_specs=[VMEM] * 10,
         scratch_shapes=[
             pltpu.VMEM(dims, kind)
-            for dims, kind in ring + [(half, BF16)] * 8 + weights + rows + blocks * 2 + parts
+            for dims, kind in ring + [(half, BF16)] * 8 + weights + rows + blocks * 2 + parts * 2
         ]
-        + [sem((3, 32)), sem((3,)), sem((7, 16)), sem((7,)), sem((3, 4)), sem((3,)), sem((3,))]
-        + [sem((2, 4, 5)), sem((2, 4, 5)), sem((2, 2, 8)), sem((2, 2)), sem((6,))],
+        + [sem((5, 64)), sem((5,)), sem((9, 16)), sem((9,)), sem((3, 4)), sem((3,)), sem((3,))]
+        + [sem((2, 4 * SPLIT, 5)), sem((2, 4 * SPLIT, 5)), sem((2, 2, 8)), sem((2, 2)), sem((6,))],
         compiler_params=pltpu.CompilerParams(
             collective_id=0, has_side_effects=True, vmem_limit_bytes=50 << 20
         ),
         name="main",
-    )(ids, gates, tokens, grad_out, w_gate[0], w_up[0], w_down[0])
+    )(*[pltpu.with_memory_space_constraint(a, pltpu.HBM) for a in inputs])
     home = [a.reshape(128, *a.shape[3:]) for a in home]
-    sums = (land_gate, land_up, land_down)
-    wide = shape(1, 256, 384, dtype=F32)
-    grad_tokens, grad_gate, *grads = local(
+    sums = (sum_gate, sum_up, sum_down)
+    args = (my_ids, my_gates, *home, *sums)
+    hbm = pl.BlockSpec(memory_space=pltpu.HBM)
+    grad_tokens, grad_gate, *grads = pl.pallas_call(
         combine_kernel,
-        (shape(128, 1024), shape(4, 128), wide, wide, shape(1, 384, 256, dtype=F32)),
-        (ids, gates, *home, *sums),
+        out_shape=[shape(128, 1024), shape(4, 128)] + [shape(*d, dtype=kind) for d, kind in totals],
+        in_specs=[VMEM] * len(args),
+        out_specs=[VMEM, VMEM, hbm, hbm, hbm],
+        scratch_shapes=[sem((3,))],
+        compiler_params=pltpu.CompilerParams(vmem_limit_bytes=24 << 20),
         name="combine",
-    )
+    )(*args)
     return (grad_tokens, grad_gate.T, *grads)
 
 

time: 135 us -> 128 us (0.948)
  local copies, waits for them, and re-layouts: 3.7 us -> 0 us
  Pallas kernels: 130 us -> 127 us
    unnamed x10 -> x0, local copies, waits for them, and re-layouts: 3.7 us -> none
    pallas_call x1, Pallas kernels: 127 us -> 124 us  [shards(): pl.pallas_call(main_kernel, out_shape=[shape(*dims, dtype=kind) for dims,...]
where the time goes in v5:
time: 128 us
  Pallas kernels  127 us (99%)
    pallas_call x1, Pallas kernels, shards(): pl.pallas_call(main_kernel, out_shape=[shape(*dims, dtype=kind) for dims,...  124 us
    pallas_call x1, Pallas kernels, shards(): pl.pallas_call(combine_kernel, out_shape=[shape(128, 1024), shape(4, 128)...  2.76 us

profile of v5, /device:TPU:1, one launch (start us, length us, event | category | flops | bytes accessed | tf_op | source)
XLA Modules:
  0.0 127.5 jit_solution(12523642841824796400)
XLA Ops:
  0.6 124.1 %main.1 = (bf16[8,8,2,8,256]{4,3,2,1,0:T(8,128)(2,1)S(1)}, bf16[8,8,2,8,256]{4,3,2,1,0:T(8,128)(2,1)S(1)}, bf16[8,8,2,8,128]{4,3,2,1,0:T(8,128)(2,1)S(1)}, bf16[...) custom-call(s32[4,128]{1,0:T(4,128)} %bitcast.19, ...), custom_call_target="tpu_custom_call" | custom-call | tf_op jit(solution)/shard_map/main/pallas_call | solution.py:585
  124.8 2.8 %combine.1 = (bf16[128,1024]{1,0:T(8,128)(2,1)}, bf16[4,128]{1,0:T(4,128)(2,1)}, f32[1,256,384]{2,1,0:T(8,128)}, f32[1,256,384]{2,1,0:T(8,128)}, f32[1,384,256]{2,1,0:T(8,128)}) custom-call(s32[4,128]{1,0:T(4,128)S(1)} %get-tuple-element.20.ids_ref, bf16[4,128]{1,0:T(4,128)(2,1)S(1)} %get-tuple-element.21.gate_ref, bf16[128,8,256]{2,1,0:T(8,128)(2,1)S(1)} %bitcast.11, ...), custom_call_target="tpu_custom_call" | custom-call | tf_op jit(solution)/shard_map/combine/pallas_call | solution.py:605

commit v6 on v5

--- a/solution.py
+++ b/solution.py
@@ -12,7 +12,7 @@
 BLOCK = 8
 ROWS = 1024
 CH = 256
-SPLIT = 1
+SPLIT = 2
 VMEM = pl.BlockSpec(memory_space=pltpu.VMEM)
 
 
@@ -40,7 +40,7 @@
     tails = [
         jnp.where((ranks == 3.0 * (place - 6.0) + j) & (place > 5.5), 1.0, 0.0) for j in range(3)
     ]
-    return rank, main, tails, spread
+    return rank, main.astype(BF16), [tail.astype(BF16) for tail in tails]
 
 
 def put_chunk(pieces, pair, j, rows):
@@ -54,36 +54,21 @@
             (third if j else first)[at] = half.reshape(8, 2, BLOCK, CH)
 
 
-def get_chunk(pieces, j):
-    first, third, low, high = pieces
-    if j == 1:
-        return jnp.concatenate(
-            [low[...].reshape(ROWS, 128), high[...].reshape(ROWS, 128)], axis=1
-        )
-    return (third if j else first)[...].reshape(ROWS, CH)
-
-
-def combine_kernel(
-    ids_ref, gate_ref, *refs
-):
-    pieces, p_ref, sums = refs[:4], refs[4], refs[5:8]
-    tok_ref, gate_out_ref, *grads = refs[8:13]
-    copies = [pltpu.make_async_copy(sums[i], grads[i], refs[13].at[i]) for i in range(3)]
+def combine_kernel(*refs):
+    ids, gates = refs[0][...], refs[1][...].astype(F32)
+    low, high, p_ref, early, last, rank, main, tail = refs[2:10]
+    sums, (tok_ref, gate_out_ref), grads, sem = refs[10:13], refs[13:15], refs[15:18], refs[18]
+    copies = [pltpu.make_async_copy(sums[i], grads[i], sem.at[i]) for i in range(3)]
     for copy in copies:
         copy.start()
-    ids = ids_ref[...]
-    rank, main, tails, _ = one_hots(ids)
-    main = main.astype(BF16)
-    last = jnp.zeros((128, CH), F32)
-    for j in range(3):
-        part = get_chunk(pieces, j)
-        tok_ref[:, j * CH : (j + 1) * CH] = dot(main, part, ((0,), (0,))).astype(BF16)
-        last = last + dot(tails[j].astype(BF16), part, ((0,), (0,)))
-    tok_ref[:, 3 * CH :] = last.astype(BF16)
+    part = jnp.concatenate([low[...].reshape(ROWS, 128), high[...].reshape(ROWS, 128)], axis=1)
+    tok_ref[:, :CH] = early[:, :CH]
+    tok_ref[:, CH : 2 * CH] = dot(main[...], part, ((0,), (0,))).astype(BF16)
+    tok_ref[:, 2 * CH : 3 * CH] = early[:, CH:]
+    tok_ref[:, 3 * CH :] = (last[...] + dot(tail[...], part, ((0,), (0,)))).astype(BF16)
     mine = jnp.zeros((128, 128), F32)
     for r in range(SLOTS):
-        mine = mine + jnp.where(rank == r, p_ref[:, 0, r : r + 1], 0.0)
-    gates = gate_ref[...].astype(F32)
+        mine = mine + jnp.where(rank[...] == r, p_ref[:, 0, r : r + 1], 0.0)
     experts = iota((128, 128), 0)
     for k in range(4):
         total = jnp.sum(jnp.where(ids[k : k + 1, :] == experts, mine, 0.0), axis=0, keepdims=True)
@@ -93,7 +78,7 @@
 
 
 def ring_step(i):
-    return jnp.where(i % 2 == 1, (i + 1) // 2, 8 - i // 2)
+    return jnp.where(i % 2 == 1, 4 - i // 2, 4 + i // 2)
 
 
 class Exchange:
@@ -295,7 +280,7 @@
                 device_id_type=pl.DeviceIdType.MESH,
             )
 
-    def pick(self, block, ids, gates):
+    def pick(self, block, ids, gates, parts=(0, 1)):
         row = iota((128, 128), 0)
         place, receiver = (row % BLOCK).astype(F32), row // BLOCK
         if self.number:
@@ -314,31 +299,35 @@
 
         def chunk(j):
             return jnp.concatenate(
-                [held[block, part, :, j * 128 : (j + 1) * 128] for part in range(2)], axis=1
+                [held[block, part, :, j * 128 : (j + 1) * 128] for part in parts], axis=1
             )
 
         last = chunk(3)
         for j in range(3):
             tail = jnp.where((rank == 3.0 * (place - 6.0) + j) & (place > 5.5), 1.0, 0.0)
-            scale = jnp.sum((main + tail) * gate, axis=1, keepdims=True)
             choice = jnp.concatenate([main.astype(BF16), tail.astype(BF16)], axis=1)
             rows = dot(choice, jnp.concatenate([chunk(j), last], axis=0))
             lanes = slice(j * 128, (j + 1) * 128)
-            self.xs[block, :, :, :, lanes] = rows[:, :128].astype(BF16).reshape(8, 2, 8, 128)
-            self.ss[block, :, :, :, lanes] = (
-                (rows[:, 128:] * scale).astype(BF16).reshape(8, 2, 8, 128)
-            )
-
-    def pick_step(self, way, step):
+            if 0 in parts:
+                self.xs[block, :, :, :, lanes] = rows[:, :128].astype(BF16).reshape(8, 2, 8, 128)
+            if 1 in parts:
+                scale = jnp.sum((main + tail) * gate, axis=1, keepdims=True)
+                self.ss[block, :, :, :, lanes] = (
+                    (rows[:, -128:] * scale).astype(BF16).reshape(8, 2, 8, 128)
+                )
+
+    def pick_step(self, way, step, parts=(0, 1)):
         block = (self.at - way * step + 8) % 8
-        self.pick(block, self.held_ids[block], self.held_gates[block].astype(F32))
+        self.pick(block, self.held_ids[block], self.held_gates[block].astype(F32), parts)
 
 
 def main_kernel(*refs):
     refs = list(refs)
     take = lambda count: [refs.pop(0) for _ in range(count)]
     (ids, gates), inputs, weights_hbm = take(2), take(2), take(3)
-    homes, sums, (my_ids, my_gates) = take(5), take(3), take(2)
+    late, sums, (my_ids, my_gates) = take(3), take(3), take(2)
+    early, last_s, rank_s, main_s, tail_s = take(5)
+    homes = take(2) + late
     helds, held_ids, held_gates = take(2), take(2), take(2)
     mids, gots, weights = take(4), take(4), take(3)
     x_s, s_s, a_s, silu_s, dg_s, du_s, h_s = take(7)
@@ -398,7 +387,7 @@
             for ring in rings:
                 for way in (1, -1):
                     ring.arrived(q, way, step - 1)
-                    if step < 4 or (way > 0) == (q < SPLIT):
+                    if step < 4 or (way > 0) == (q % 2 == 0):
                         ring.copy(q, way, step).start()
         for ring in rings:
             if step == 2:
@@ -407,10 +396,16 @@
             for way in (1, -1):
                 ring.pick_step(way, step - 1)
     for ring in rings:
-        for q in pieces:
-            ring.arrived(q, 1 if q < SPLIT else -1, 4)
-        ring.pick_step(1, 4)
-    for stream in outward:
+        for q in pieces[:SPLIT]:
+            ring.arrived(q, 1 if q % 2 == 0 else -1, 4)
+        ring.pick_step(1, 4, (0,))
+    for stream in outward[:2]:
+        stream.phase2(received=False)
+    for ring in rings:
+        for q in pieces[SPLIT:]:
+            ring.arrived(q, 1 if q % 2 == 0 else -1, 4)
+        ring.pick_step(1, 4, (1,))
+    for stream in outward[2:]:
         stream.phase2(received=False)
 
     row, col = iota((CH, CH), 0), iota((CH, CH), 1)
@@ -437,8 +432,8 @@
     z = me // 16
 
     def pair_of(g):
-        far = jnp.where(g < 3, 3 - g, 4)
-        return (z + far) % 8, (z + jnp.where(g < 3, 8 - far, 0)) % 8
+        far = 4 - g
+        return (z + far) % 8, (z + jnp.where(g > 0, 8 - far, 0)) % 8
 
     def unpack_group(halves, ref, g):
         rows, pair = rows_of(g), pair_of(g)
@@ -543,7 +538,17 @@
     for k in range(3):
         pltpu.make_async_copy(lands[k], lands[k], recv3.at[k]).wait()
         sums[k][0] = sum(lands[k][i].astype(F32) for i in range(1, 4)) + lands[k][0].astype(F32)
-    for stream in homeward:
+    rank, main, tails = one_hots(my_ids[...])
+    rank_s[...] = rank
+    main_s[...] = main
+    tail_s[...] = tails[1]
+    for stream in homeward[:2]:
+        stream.arrived()
+    first, third = homes[0][...].reshape(ROWS, CH), homes[1][...].reshape(ROWS, CH)
+    early[:, :CH] = dot(main, first, ((0,), (0,))).astype(BF16)
+    early[:, CH:] = dot(main, third, ((0,), (0,))).astype(BF16)
+    last_s[...] = dot(tails[0], first, ((0,), (0,))) + dot(tails[2], third, ((0,), (0,)))
+    for stream in homeward[2:]:
         stream.arrived()
     for ring in rings:
         for i in range(1, 8):
@@ -552,7 +557,7 @@
         for step in range(1, 5):
             for q in pieces:
                 for way in (1, -1):
-                    if step < 4 or (way > 0) == (q < SPLIT):
+                    if step < 4 or (way > 0) == (q % 2 == 0):
                         ring.copy(q, way, step).wait_send()
     for stream in outward:
         stream.sent2()
@@ -581,15 +586,17 @@
     ring = [((8, 2, 128, 512), BF16)] * 2 + [((8, 4, 128), jnp.int32)] * 2
     ring += [((8, 4, 128), BF16)] * 2
     routes = [((4, 128), jnp.int32), ((4, 128), BF16)]
+    combine = [((128, 2 * CH), BF16), ((128, CH), F32), ((128, 128), F32)]
+    combine += [((ROWS, 128), BF16)] * 2
     sem = pltpu.SemaphoreType.DMA
-    *home, sum_gate, sum_up, sum_down, my_ids, my_gates = pl.pallas_call(
+    outs = pl.pallas_call(
         main_kernel,
-        out_shape=[shape(*dims, dtype=kind) for dims, kind in blocks + totals + routes],
+        out_shape=[shape(*dims, dtype=kind) for dims, kind in blocks[2:] + totals + routes + combine],
         in_specs=[pl.BlockSpec(memory_space=pltpu.HBM)] * 7,
-        out_specs=[VMEM] * 10,
+        out_specs=[VMEM] * 13,
         scratch_shapes=[
             pltpu.VMEM(dims, kind)
-            for dims, kind in ring + [(half, BF16)] * 8 + weights + rows + blocks * 2 + parts * 2
+            for dims, kind in blocks[:2] + ring + [(half, BF16)] * 8 + weights + rows + blocks * 2 + parts * 2
         ]
         + [sem((5, 64)), sem((5,)), sem((9, 16)), sem((9,)), sem((3, 4)), sem((3,)), sem((3,))]
         + [sem((2, 4 * SPLIT, 5)), sem((2, 4 * SPLIT, 5)), sem((2, 2, 8)), sem((2, 2)), sem((6,))],
@@ -598,9 +605,8 @@
         ),
         name="main",
     )(*[pltpu.with_memory_space_constraint(a, pltpu.HBM) for a in inputs])
-    home = [a.reshape(128, *a.shape[3:]) for a in home]
-    sums = (sum_gate, sum_up, sum_down)
-    args = (my_ids, my_gates, *home, *sums)
+    late = [a.reshape(128, *a.shape[3:]) for a in outs[:3]]
+    args = (*outs[6:8], *late, *outs[8:], *outs[3:6])
     hbm = pl.BlockSpec(memory_space=pltpu.HBM)
     grad_tokens, grad_gate, *grads = pl.pallas_call(
         combine_kernel,

time: 128 us -> 126 us (0.984)
  Pallas kernels: 127 us -> 125 us
where the time goes in v6:
time: 126 us
  Pallas kernels  125 us (99%)
    pallas_call x1, Pallas kernels, shards(): pl.pallas_call(main_kernel, out_shape=[shape(*dims, dtype=kind) for dims,...  123 us

profile of v6, /device:TPU:1, one launch (start us, length us, event | category | flops | bytes accessed | tf_op | source)
XLA Modules:
  0.0 125.6 jit_solution(5486840091716315157)
XLA Ops:
  0.6 123.0 %main.1 = (bf16[8,8,2,8,128]{4,3,2,1,0:T(8,128)(2,1)S(1)}, bf16[8,8,2,8,128]{4,3,2,1,0:T(8,128)(2,1)S(1)}, f32[8,8,2,1,128]{4,3,2,1,0:T(1,128)S(1)}, f32[1,256,3...) custom-call(s32[4,128]{1,0:T(4,128)} %bitcast.15, ...), custom_call_target="tpu_custom_call" | custom-call | tf_op jit(solution)/shard_map/main/pallas_call | solution.py:592
  123.6 1.9 %combine.1 = (bf16[128,1024]{1,0:T(8,128)(2,1)}, bf16[4,128]{1,0:T(4,128)(2,1)}, f32[1,256,384]{2,1,0:T(8,128)}, f32[1,256,384]{2,1,0:T(8,128)}, f32[1,384,256]{2,1,0:T(8,128)}) custom-call(s32[4,128]{1,0:T(4,128)S(1)} %get-tuple-element.23.refs_0_, bf16[4,128]{1,0:T(4,128)(2,1)S(1)} %get-tuple-element.24.refs_1_, bf16[128,8,128]{2,1,0:T(8,128)(2,1)S(1)} %bitcast.9, ...), custom_call_target="tpu_custom_call" | custom-call | tf_op jit(solution)/shard_map/combine/pallas_call | solution.py:611

commit v7 on v6

--- a/solution.py
+++ b/solution.py
@@ -479,6 +479,11 @@
         hgrad = dot(s_s[rows, :], wd[...], ((1,), (1,)))
         d_gate = (hgrad * a_s[rows, :]).astype(BF16)
         d_up = (hgrad * silu_s[rows, :]).astype(BF16)
+        @pl.when(g > 0)
+        def _():
+            for stream in homeward[:2]:
+                stream.group1(pair_of(g - 1))
+
         dg_s[rows, :] = d_gate
         du_s[rows, :] = d_up
         product = jnp.sum(h_s[rows, :].astype(F32) * hgrad, axis=1, keepdims=True)
@@ -495,11 +500,6 @@
             part = route(slice(j * CH, (j + 1) * CH)) + dot(repack[j], tail)
             put_chunk(backs[:4], pair, j, part.astype(BF16))
 
-        @pl.when(g > 0)
-        def _():
-            for stream in homeward[:2]:
-                stream.group1(pair_of(g - 1))
-
         return 0
 
     lax.fori_loop(0, 4, backward, 0)
@@ -512,11 +512,12 @@
         parts[2][i] = dot(h_s[...], s_s[:, cols], ((0,), (0,))).astype(BF16)
         return 0
 
-    lax.fori_loop(0, 4, grads, 0)
+    lax.fori_loop(0, 1, grads, 0)
     for stream in homeward[:2]:
         stream.group1(pair_of(3))
     for stream in homeward[2:]:
         stream.phase1()
+    lax.fori_loop(1, 4, grads, 0)
 
     def scatter_copy(k, i):
         target = (dp + i) % 4

time: 126 us -> 127 us (level)
  no operation moved by 1% of the time
where the time goes in v7:
time: 127 us; the launch traced here: 126 us
  Pallas kernels  126 us (99%)
    pallas_call x1, Pallas kernels, shards(): pl.pallas_call(main_kernel, out_shape=[shape(*dims, dtype=kind) for dims,...  124 us

profile of v7, /device:TPU:1, one launch (start us, length us, event | category | flops | bytes accessed | tf_op | source)
XLA Modules:
  0.0 126.4 jit_solution(2870452548193478699)
XLA Ops:
  0.6 123.7 %main.1 = (bf16[8,8,2,8,128]{4,3,2,1,0:T(8,128)(2,1)S(1)}, bf16[8,8,2,8,128]{4,3,2,1,0:T(8,128)(2,1)S(1)}, f32[8,8,2,1,128]{4,3,2,1,0:T(1,128)S(1)}, f32[1,256,3...) custom-call(s32[4,128]{1,0:T(4,128)} %bitcast.15, ...), custom_call_target="tpu_custom_call" | custom-call | tf_op jit(solution)/shard_map/main/pallas_call | solution.py:593
  124.3 1.9 %combine.1 = (bf16[128,1024]{1,0:T(8,128)(2,1)}, bf16[4,128]{1,0:T(4,128)(2,1)}, f32[1,256,384]{2,1,0:T(8,128)}, f32[1,256,384]{2,1,0:T(8,128)}, f32[1,384,256]{2,1,0:T(8,128)}) custom-call(s32[4,128]{1,0:T(4,128)S(1)} %get-tuple-element.23.refs_0_, bf16[4,128]{1,0:T(4,128)(2,1)S(1)} %get-tuple-element.24.refs_1_, bf16[128,8,128]{2,1,0:T(8,128)(2,1)S(1)} %bitcast.9, ...), custom_call_target="tpu_custom_call" | custom-call | tf_op jit(solution)/shard_map/combine/pallas_call | solution.py:612
